TPU v7x, 32 devices: a whole 2x2x4 slice. The times are simulated.
32 devices in a mesh: dp: 8 (over z, x), seq: 4 (over y, core).
Axes of the slice: x: 2, y: 2, z: 4, core: 2. Of those that a mesh axis runs over, the one named last changes fastest.
Arguments:
- hidden: bfloat16 [8, 1024, 1536], P('dp', 'seq'), may hold values from -6 to 6
- segments: int32 [8, 1024], P('dp', 'seq'), may hold values from 0 to 3, never falling along the last dimension, each value on 1 to 768 neighbouring positions
- cotangent: bfloat16 [8, 1024, 1536], P('dp', 'seq'), may hold values from -6 to 6
- norm_gain: float32 [1536], replicated, may hold values from 0.5 to 1.5
- in_weight: float32 [1536, 6448], P(('dp', 'seq')), may hold values from -0.15625 to 0.15625
- conv_weight: float32 [4, 3328], replicated, may hold values from -3 to 3
- conv_bias: float32 [3328], replicated, may hold values from -3 to 3
- step_bias: float32 [48], replicated, may hold values from -4 to -1
- log_rate: float32 [48], replicated, may hold values from -5 to 0.5
- skip_gain: float32 [48], replicated, may hold values from 0.5 to 1.5
- gate_gain: float32 [3072], replicated, may hold values from 0.5 to 1.5
- out_weight: float32 [3072, 1536], P(('dp', 'seq')), may hold values from -0.109375 to 0.109375
Outputs:
- result: bfloat16 [8, 1024, 1536], P('dp', 'seq')
- d_hidden: float32 [8, 1024, 1536], P('dp', 'seq')
- d_norm_gain: float32 [1536], replicated
- d_in_weight: float32 [1536, 6448], P(('dp', 'seq'))
- d_conv_weight: float32 [4, 3328], replicated
- d_conv_bias: float32 [3328], replicated
- d_step_bias: float32 [48], replicated
- d_log_rate: float32 [48], replicated
- d_skip_gain: float32 [48], replicated
- d_gate_gain: float32 [3072], replicated
- d_out_weight: float32 [3072, 1536], P(('dp', 'seq'))
Inputs may be any that keep to these rules, and one draw needn't show every extreme that they name: `segments`: along each sequence the numbers never fall; a document is a run of equal numbers of 1 to 768 tokens, and one run holds exactly 768.
All inputs are finite; a program needn't handle non-finite values.
Results may differ from a plain program's by a relative error of at most 0.0096.
Values may be sent and summed in bfloat16 or wider, within the bound.
No kernel may reach another device: no remote copies, remote signals or barrier semaphores. Data moves between devices by JAX's collectives and lax.ppermute only.
A program may use at most 256 MiB of HBM per device.

v0:
```python
import jax
import jax.numpy as jnp
from jax import lax
from jax.sharding import PartitionSpec as P

epsilon = 1e-05
highest = lax.Precision.HIGHEST


def passed_along(block, axis, distance):
    devices = range(lax.axis_size(axis))
    route = [(i - distance, i) for i in devices if i - distance in devices]
    return lax.ppermute(block, axis, route)


def carried_in(value, axis, combine, identity, reverse):
    count, index = (lax.axis_size(axis), lax.axis_index(axis))
    everything = jax.tree.map(lambda part: lax.all_gather(part, axis), value)
    start = jax.tree.map(
        lambda part, zero: jnp.broadcast_to(jnp.asarray(zero, part.dtype), part.shape),
        value,
        identity,
    )

    def hop(k, before):
        at = count - 1 - k if reverse else k
        reached = at > index if reverse else at < index
        new = combine(before, jax.tree.map(lambda part: part[at], everything))
        return jax.tree.map(lambda a, b: jnp.where(reached, a, b), new, before)

    return lax.fori_loop(0, count, hop, start)


def rms_scale(values, scaling):
    mean_sq = jnp.mean(values * values, axis=-1, keepdims=True)
    return values * lax.rsqrt(mean_sq + epsilon) * scaling


def add_skip(ssd_out, x_part, skip_gain):
    dims_of = ssd_out.shape
    n_heads = skip_gain.shape[0]
    grouped = ssd_out.reshape(dims_of[:-1] + (n_heads, -1)) + skip_gain[:, None] * x_part.reshape(
        dims_of[:-1] + (n_heads, -1)
    )
    return grouped.reshape(dims_of)


def conv_mixer(extended, doc_ext, conv_weight, conv_bias, step_raw, step_bias, log_rate):
    n_taps = conv_weight.shape[0]
    block = extended.shape[1] - (n_taps - 1)
    own_ids = doc_ext[:, n_taps - 1 :]
    running = conv_bias + conv_weight[0] * extended[:, n_taps - 1 :, :]
    for offset in range(1, n_taps):
        begin_at = n_taps - 1 - offset
        same_doc = jnp.where(doc_ext[:, begin_at : begin_at + block] == own_ids, 1.0, 0.0)
        running = (
            running
            + conv_weight[offset]
            * extended[:, begin_at : begin_at + block, :]
            * same_doc[:, :, None]
        )
    activated = jax.nn.silu(running)
    step_size = jax.nn.softplus(step_raw + step_bias)
    log_decay = -step_size * jnp.exp(log_rate)
    return (activated, step_size, log_decay)


def block_inner(x_part, b_part, c_part, step_size, log_decay, doc_ids):
    block, n_heads = step_size.shape
    x_heads = x_part.reshape(block, n_heads, -1)
    cumulative = jnp.cumsum(log_decay, axis=0)
    cum_heads = cumulative.T
    position = jnp.arange(block)
    causal = jnp.logical_and(
        position[:, None] >= position[None, :], doc_ids[:, None] == doc_ids[None, :]
    )
    log_gap = jnp.where(causal[None], cum_heads[:, :, None] - cum_heads[:, None, :], 0.0)
    scores = jnp.dot(c_part, b_part.T, precision=highest)
    weights = (
        jnp.where(causal[None], jnp.exp(log_gap), 0.0) * scores[None] * step_size.T[:, None, :]
    )
    output = jnp.einsum("hts,shp->thp", weights, x_heads, precision=highest)
    to_end = (
        jnp.where(doc_ids == doc_ids[-1], 1.0, 0.0)[:, None]
        * jnp.exp(cumulative[-1][None, :] - cumulative)
        * step_size
    )
    carried = jnp.einsum("sh,shp,sn->hpn", to_end, x_heads, b_part, precision=highest)
    return (output.reshape(block, -1), carried, jnp.exp(cumulative[-1]))


def block_enter(c_part, log_decay, doc_ids, state_in, id_in):
    cumulative = jnp.cumsum(log_decay, axis=0)
    entering = jnp.where(doc_ids == id_in, 1.0, 0.0)[:, None] * jnp.exp(cumulative)
    output = jnp.einsum("tn,hpn->thp", c_part, state_in, precision=highest) * entering[:, :, None]
    return output.reshape(c_part.shape[0], -1)


def link_states(earlier, later):
    fade_early, state_early, last_early = earlier
    fade_late, state_late, last_late = later
    is_empty = last_late < 0.0
    linked = jnp.where(jnp.logical_or(is_empty, last_late == last_early), 1.0, 0.0)
    kept_share = linked[:, None] * fade_late
    merged = state_late + kept_share[:, :, None, None] * state_early
    return (fade_early * fade_late, merged, jnp.where(is_empty, last_early, last_late))


def pass_back(earlier, later):
    factor_high, grad_high = earlier
    factor_low, grad_low = later
    return (factor_low * factor_high, grad_low + factor_low[:, :, None, None] * grad_high)


def shards(
    hidden,
    segments,
    cotangent,
    norm_gain,
    in_weight,
    conv_weight,
    conv_bias,
    step_bias,
    log_rate,
    skip_gain,
    gate_gain,
    out_weight,
):
    n_seqs, block, n_width = hidden.shape
    n_rows = n_seqs * block
    n_inner = gate_gain.shape[0]
    n_heads = step_bias.shape[0]
    n_taps = conv_weight.shape[0]
    n_mixed = conv_bias.shape[0]
    n_state = (n_mixed - n_inner) // 2
    contract_rows = (((0,), (0,)), ((), ()))
    contract_cols = (((1,), (1,)), ((), ()))
    flat = hidden.reshape(n_rows, n_width).astype(jnp.float32)
    normed, norm_pull = jax.vjp(rms_scale, flat, norm_gain)
    normed_low = normed.astype(jnp.bfloat16)
    in_low = in_weight.astype(jnp.bfloat16)
    out_low = out_weight.astype(jnp.bfloat16)
    in_full = lax.all_gather(in_low, ("dp", "seq"), axis=0, tiled=True)
    projected = jnp.dot(normed_low, in_full, preferred_element_type=jnp.float32)
    gate_z = projected[:, :n_inner].reshape(n_seqs, block, n_inner)
    conv_low = (
        projected[:, n_inner : n_inner + n_mixed]
        .astype(jnp.bfloat16)
        .reshape(n_seqs, block, n_mixed)
    )
    step_raw = projected[:, n_inner + n_mixed :].reshape(n_seqs, block, n_heads)
    doc_ids = segments.astype(jnp.float32)
    edge = block - (n_taps - 1)
    prev_rows, prev_ids = passed_along(
        (conv_low[:, edge:, :], doc_ids[:, edge:].astype(jnp.bfloat16)), "seq", 1
    )
    extended = jnp.concatenate([prev_rows, conv_low], axis=1).astype(jnp.float32)
    doc_ext = jnp.concatenate([prev_ids.astype(jnp.float32), doc_ids], axis=1)

    def mixer_in(ext_values, weights_conv, bias_conv, raw_steps, bias_steps, rate_logs):
        return conv_mixer(
            ext_values, doc_ext, weights_conv, bias_conv, raw_steps, bias_steps, rate_logs
        )

    (activated, step_size, log_decay), mixer_pull = jax.vjp(
        mixer_in, extended, conv_weight, conv_bias, step_raw, step_bias, log_rate
    )
    x_part = activated[..., :n_inner]
    b_part = activated[..., n_inner : n_inner + n_state]
    c_part = activated[..., n_inner + n_state :]

    def inner_all(x_values, b_values, c_values, steps, decays):
        return jax.vmap(block_inner)(x_values, b_values, c_values, steps, decays, doc_ids)

    (inner_out, local_state, retained), inner_pull = jax.vjp(
        inner_all, x_part, b_part, c_part, step_size, log_decay
    )
    last_ids = doc_ids[:, -1]
    identity = (jnp.ones_like(retained), jnp.zeros_like(local_state), -jnp.ones_like(last_ids))
    fade_in, state_in, id_in = carried_in(
        (retained, local_state, last_ids), "seq", link_states, identity, False
    )

    def enter_all(c_values, decays, incoming):
        return jax.vmap(block_enter)(c_values, decays, doc_ids, incoming, id_in)

    enter_out, enter_pull = jax.vjp(enter_all, c_part, log_decay, state_in)
    ssd_out = inner_out + enter_out

    def gate_tail(ssd_values, x_values, skip_values, gate_values, scaling):
        return rms_scale(
            add_skip(ssd_values, x_values, skip_values) * jax.nn.silu(gate_values), scaling
        )

    gate_normed, gate_pull = jax.vjp(gate_tail, ssd_out, x_part, skip_gain, gate_z, gate_gain)
    gate_low = gate_normed.reshape(n_rows, n_inner).astype(jnp.bfloat16)
    out_full = lax.all_gather(out_low, ("dp", "seq"), axis=0, tiled=True)
    branch_out = jnp.dot(gate_low, out_full, preferred_element_type=jnp.float32)
    result = (flat + branch_out).reshape(n_seqs, block, n_width).astype(jnp.bfloat16)
    cot_rows = cotangent.reshape(n_rows, n_width)
    out_term = lax.dot_general(
        gate_low, cot_rows, contract_rows, preferred_element_type=jnp.float32
    )
    d_out_weight = lax.psum_scatter(out_term, ("dp", "seq"), scatter_dimension=0, tiled=True)
    out_used = lax.all_gather(out_low, ("dp", "seq"), axis=0, tiled=True)
    d_gate_normed = lax.dot_general(
        cot_rows, out_used, contract_cols, preferred_element_type=jnp.float32
    )
    d_ssd, d_x_skip, d_skip_gain, d_gate_z, d_gate_gain = gate_pull(
        d_gate_normed.reshape(n_seqs, block, n_inner)
    )
    d_c_enter, d_decay_enter, grad_state = enter_pull(d_ssd)
    linked = jnp.where(last_ids == id_in, 1.0, 0.0)
    factor_out = linked[:, None] * retained
    back_identity = (jnp.ones_like(factor_out), jnp.zeros_like(grad_state))
    grad_after = carried_in((factor_out, grad_state), "seq", pass_back, back_identity, True)[1]
    d_retained = linked[:, None] * jnp.sum(grad_after * state_in, axis=(2, 3))
    d_x_inner, d_b_part, d_c_inner, d_step_inner, d_decay_inner = inner_pull(
        (d_ssd, grad_after, d_retained)
    )
    d_activated = jnp.concatenate([d_x_inner + d_x_skip, d_b_part, d_c_inner + d_c_enter], axis=-1)
    d_extended, d_conv_weight, d_conv_bias, d_step_raw, d_step_bias, d_log_rate = mixer_pull(
        (d_activated, d_step_inner, d_decay_inner + d_decay_enter)
    )
    returned = passed_along(d_extended[:, : n_taps - 1, :].astype(jnp.bfloat16), "seq", -1).astype(
        jnp.float32
    )
    d_own = d_extended[:, n_taps - 1 :, :]
    d_conv_in = jnp.concatenate([d_own[:, :edge, :], d_own[:, edge:, :] + returned], axis=1)
    d_projected = jnp.concatenate(
        [
            d_gate_z.reshape(n_rows, n_inner),
            d_conv_in.reshape(n_rows, n_mixed),
            d_step_raw.reshape(n_rows, n_heads),
        ],
        axis=1,
    ).astype(jnp.bfloat16)
    in_term = lax.dot_general(
        normed_low, d_projected, contract_rows, preferred_element_type=jnp.float32
    )
    d_in_weight = lax.psum_scatter(in_term, ("dp", "seq"), scatter_dimension=0, tiled=True)
    in_used = lax.all_gather(in_low, ("dp", "seq"), axis=0, tiled=True)
    d_normed = lax.dot_general(
        d_projected, in_used, contract_cols, preferred_element_type=jnp.float32
    )
    d_flat, d_norm_gain = norm_pull(d_normed)
    d_hidden = (cot_rows.astype(jnp.float32) + d_flat).reshape(n_seqs, block, n_width)
    summed = lax.psum(
        (
            d_norm_gain,
            d_conv_weight,
            d_conv_bias,
            d_step_bias,
            d_log_rate,
            d_skip_gain,
            d_gate_gain,
        ),
        ("dp", "seq"),
    )
    return (
        result,
        d_hidden,
        summed[0],
        d_in_weight,
        summed[1],
        summed[2],
        summed[3],
        summed[4],
        summed[5],
        summed[6],
        d_out_weight,
    )


def solution(mesh):
    return jax.shard_map(
        shards,
        mesh=mesh,
        in_specs=(
            P("dp", "seq", None),
            P("dp", "seq"),
            P("dp", "seq", None),
            P(),
            P(("dp", "seq"), None),
            P(),
            P(),
            P(),
            P(),
            P(),
            P(),
            P(("dp", "seq"), None),
        ),
        out_specs=(
            P("dp", "seq", None),
            P("dp", "seq", None),
            P(),
            P(("dp", "seq"), None),
            P(),
            P(),
            P(),
            P(),
            P(),
            P(),
            P(("dp", "seq"), None),
        ),
        check_vma=False,
    )
```

profile of v0, /device:TPU:2, one launch (start us, length us, event | category | flops | bytes accessed | tf_op | source)
XLA Modules:
  0.0 1306.4 jit_solution(17510120028564940175)
XLA Ops:
  16.6 125.5 %all-gather.7.cloned.1.call-done = bf16[1536,6448]{1,0:T(8,128)(2,1)} async-done(((bf16[48,6448]{1,0:T(8,128)(2,1)}), bf16[1536,6448]{1,0:T(8,128)(2,1)}) %all-gather.7.cloned.1.call-update) | async-done | bytes 19808272 | tf_op jit(solution)/shard_map/all_gather | solution.py:143
  142.2 14.8 %fusion.75 = f32[256,6448]{0,1:T(8,128)} fusion(bf16[1536,6448]{1,0:T(8,128)(2,1)} %all-gather.7.cloned.1.call-done, bf16[1,256,1536]{2,1,0:T(8,128)(2,1)S(1)} %copy-done.15, f32[1536]{0:T(1024)S(1)} %copy-done.28, f32[256]{0:T(256)S(1)} %fusion.109), kind=kOutput, calls=%fused_computation.120 | convolution fusion | flops 5072486400 | bytes 27204608 | tf_op jit(solution)/shard_map/dot_general | solution.py:144
  167.7 4.4 copy.225
  172.4 6.7 maximum_convert_fusion
  179.2 17.0 %add_divide_fusion = (f32[1,256,3328]{2,0,1:T(1,128)S(1)}, f32[1,256,3328]{2,0,1:T(1,128)S(1)}) fusion(f32[256]{0:T(256)S(1)} %bitcast.348, f32[1,259,3328]{2,0,1:T(1,128)S(1)} %maximum_convert_fusion, f32[3328]{0:T(1024)S(1)} %copy-done.38, f32[256]{0:T(256)S(1)} %bitcast.351, f32[3328]{0:T(1024)S(1)} %copy-done.40, f32[256]{0:T(256)S(1)} %bitcast.345, ...), kind=kLoop, calls=%fused_computation.47 | loop fusion | flops 11927552 | bytes 20516864 | tf_op jit(solution)/shard_map/jvp(jit(silu))/div | solution.py:62
  202.7 3.5 copy.228
  206.2 5.7 fusion.37
  218.1 7.5 all-reduce.10
  227.7 3.7 slice.147
  235.3 3.5 copy.276
  238.8 6.6 all_gather.35
  248.9 8.0 all-gather.11.cloned.1.call-done
  256.9 28.3 %while.32 = (s32[]{:T(128)}, f32[1,48,64,128]{3,2,1,0:T(8,128)}, f32[1]{0:T(128)}, s32[]{:T(128)}, f32[4,1,48,64,128]{4,3,2,1,0:T(8,128)}, /*index=5*/f32[4,1]{0...) while((s32[]{:T(128)}, f32[1,48,64,128]{3,2,1,0:T(8,128)}, ...), condition=%wide.region_4.5_spmd.clone, body=%wide.region_3.4_spmd.clone.sunk | while | flops 1572922 | bytes 4719389 | solution.py:31
  267.7 3.4 fusion.139
  288.5 4.3 fusion.58
  292.9 16.8 %fusion.30 = f32[1,256,48,64]{1,3,2,0:T(8,128)} fusion(f32[1,256,48,64]{1,3,2,0:T(8,128)S(1)} %bitcast.311, f32[256,48,64]{0,2,1:T(8,128)S(1)} %fusion.58, f32[256,48,64]{0,2,1:T(8,128)S(1)} %bitcast.310, f32[48,256]{1,0:T(8,128)S(1)} %copy-done.49, f32[256,256]{1,0:T(8,128)S(1)} %copy-done.29, f32[48,256]{1,0:T(8,128)S(1)} %copy-done.50, ...), kind=kOutput, calls=%fused_computation.55 | convolution fusion | flops 2434793472 | bytes 13058240 | tf_op jit(solution)/shard_map/jvp(vmap(hts,shp->thp))/dot_general | solution.py:82
  309.7 4.1 copy.240
  315.7 3.5 copy.242
  319.3 5.5 multiply_reduce_fusion.9
  324.8 17.0 %all-gather.9.cloned.1.call-done = bf16[3072,1536]{1,0:T(8,128)(2,1)} async-done(((bf16[96,1536]{1,0:T(8,128)(2,1)}), bf16[3072,1536]{1,0:T(8,128)(2,1)}) %all-gather.9.cloned.1.call-update) | async-done | bytes 9437200 | tf_op jit(solution)/shard_map/all_gather | solution.py:197
  341.7 8.4 multiply_reduce_fusion.6
  356.3 3.7 copy.243
  360.0 5.6 fusion.88
  366.5 3.5 copy.245
  371.3 4.4 multiply_reduce_fusion.7
  376.5 22.7 %fusion.12 = (f32[48,256]{1,0:T(8,128)}, f32[48,256]{1,0:T(8,128)S(1)}, f32[48,256]{1,0:T(8,128)}, f32[256,256]{1,0:T(8,128)}) fusion(f32[48,256]{1,0:T(8,128)} %copy.233, f32[256,256]{1,0:T(8,128)} %fusion.93, f32[48,256]{1,0:T(8,128)} %bitcast_add_fusion.9, pred[256,256]{1,0:T(8,128)(4,1)} %fusion.73, f32[48,64,256]{2,1,0:T(8,128)} %bitcast.316, ...), kind=kOutput, calls=%fused_computation.19 | convolution fusion | flops 2463002624 | bytes 7127040 | tf_op jit(solution)/shard_map/transpose(jvp(vmap(hts,shp->thp)))/dot_general | solution.py:82
  403.8 5.7 all_gather.39
  411.8 7.4 fusion.65
  421.2 5.7 fusion.29
  426.9 12.9 while.33
  442.7 7.8 fusion.35
  450.4 5.2 fusion.33
  474.0 14.1 %bitcast_add_fusion.2 = f32[1,256,48,64]{1,3,2,0:T(8,128)} fusion(f32[48,64,256]{2,1,0:T(8,128)} %get-tuple-element.485, f32[48,64,256]{2,1,0:T(8,128)} %bitcast.317, f32[48,256]{1,0:T(8,128)} %copy.233, f32[256,256]{1,0:T(8,128)} %fusion.93, f32[48,256]{1,0:T(8,128)} %bitcast_add_fusion.9, pred[256,256]{1,0:T(8,128)(4,1)} %fusion.73, f32[256,48]{0,1:T(8,128)S(1)} %copy.235), kind=kOutput, calls=%fused_computation.53 | convolution fusion | flops 2433220608 | bytes 9912320 | tf_op jit(solution)/shard_map/transpose(jvp(vmap(hts,shp->thp)))/dot_general | solution.py:82
  488.1 3.6 copy.246
  491.7 5.2 multiply_add_fusion.1
  496.9 5.7 add.232
  503.7 27.5 %multiply_reduce_fusion.5 = (f32[3328]{0:T(1024)S(1)}, f32[3328]{0:T(1024)S(1)}, f32[3328]{0:T(1024)S(1)}, f32[3328]{0:T(1024)S(1)}, f32[3328]{0:T(1024)}, /*index=5*/f32[1,256,3328]{2,0,1:T(1,128)}) fusion(f32[1,259,3328]{2,0,1:T(1,128)S(1)} %maximum_convert_fusion, f32[256]{0:T(256)} %bitcast.346, f32[256]{0:T(256)} %bitcast.349, f32[256]{0:T(256)} %bitcast.343, ...), kind=kLoop, calls=%fused_computation.46 | loop fusion | flops 17022720 | bytes 27332608 | tf_op jit(solution)/shard_map/transpose(jvp())/reduce_sum | solution.py:58
  534.5 11.5 multiply_multiply_fusion.2
  546.1 7.8 fusion.120
  557.3 3.5 slice.148
  560.9 4.4 pad_maximum_fusion.1
  566.7 12.6 fusion.48
  579.4 9.1 fusion.68
  588.6 17.9 %fusion.63 = f32[1536,6448]{1,0:T(8,128)} fusion(bf16[256,48]{1,0:T(8,128)(2,1)S(1)} %bitcast.338, bf16[256,3328]{1,0:T(8,128)(2,1)} %bitcast.324, bf16[256,3072]{1,0:T(8,128)(2,1)} %fusion.29, bf16[1,256,1536]{2,1,0:T(8,128)(2,1)} %param.16, f32[1536]{0:T(1024)S(1)} %copy-done.28, f32[256]{0:T(256)S(1)} %copy-done.43), kind=kOutput, calls=%fused_computation.106 | convolution fusion | flops 5082390528 | bytes 43711488 | tf_op jit(solution)/shard_map/dot_general | solution.py:238
  606.6 7.5 fusion.40
  615.8 89.9 %all-reduce.14.cloned.1.call-done = (f32[1536]{0:T(1024)}, f32[4,3328]{1,0:T(4,128)}, f32[3328]{0:T(1024)}, f32[48]{0:T(128)}, f32[48]{0:T(128)}, /*index=5*/f32[48]{0:T(128)}, f32[3072]{0:T(1024)}) async-done(((f32[1536]{0:T(1024)}, f32[4,3328]{1,0:T(4,128)}, f32[3328]{0:T(1024)}, f32[48]{0:T(128)}, f32[48]{0:T(128)}, /*index=5*/f32[48]{0:T(128)}, f32[3072]{0:T(1024)}), (f32[1536]{0:T(1024)}, ...) | async-done | bytes 85584 | tf_op jit(solution)/shard_map/psum | solution.py:248
  705.7 214.6 %reduce-scatter.5.cloned.1.call-done = f32[96,1536]{1,0:T(8,128)} async-done(((f32[3072,1536]{1,0:T(8,128)}), f32[96,1536]{1,0:T(8,128)}) %reduce-scatter.5.cloned.1.call-update) | async-done | bytes 589840 | tf_op jit(solution)/shard_map/reduce_scatter | solution.py:204
  920.3 369.9 %reduce-scatter.3.cloned.1.call-done = f32[48,6448]{1,0:T(8,128)} async-done(((f32[1536,6448]{1,0:T(8,128)}), f32[48,6448]{1,0:T(8,128)}) %reduce-scatter.3.cloned.1.call-update) | async-done | bytes 1238032 | tf_op jit(solution)/shard_map/reduce_scatter | solution.py:241
  (295 shorter events, 135.3 us)
Async XLA Ops:
  7.2 135.0 %copy-start.28 = (f32[1536]{0:T(1024)S(1)}, f32[1536]{0:T(1024)}, u32[]{:S(2)}) copy-start(f32[1536]{0:T(1024)} %param.19) | copy-start | bytes 18436
  7.2 135.0 %all-gather.7.cloned.1.call-start = ((), (), s32[]{:S(2)}) async-start(), calls=%async_computation.2 | async-start | bytes 20680704 | tf_op jit(solution)/shard_map/all_gather | solution.py:143
  9.5 247.4 %all-gather.11.cloned.1.call-start = ((), (), s32[]{:S(2)}) async-start(), calls=%async_computation.6 | async-start | bytes 7864320 | tf_op jit(solution)/shard_map/all_gather | solution.py:18
  10.3 146.7 %copy-start.60 = (f32[1,256]{1,0:T(1,128)}, f32[1,256]{1,0:T(1,128)S(1)}, u32[]{:S(2)}) copy-start(f32[1,256]{1,0:T(1,128)S(1)} %convert_element_type.58) | copy-start | bytes 3076
  10.3 5.6 collective-permute-start.1
  13.3 144.6 %copy-start.74 = (f32[48]{0:T(128)}, f32[48]{0:T(128)S(1)}, u32[]{:S(2)}) copy-start(f32[48]{0:T(128)S(1)} %exp.49) | copy-start | bytes 580
  15.3 141.7 %copy-start.66 = (f32[256]{0:T(256)}, f32[256]{0:T(256)S(1)}, u32[]{:S(2)}) copy-start(f32[256]{0:T(256)S(1)} %fusion.51) | copy-start | bytes 3076
  15.3 126.9 %copy-start.42 = (f32[256]{0:T(256)}, f32[256]{0:T(256)S(1)}, u32[]{:S(2)}) copy-start(f32[256]{0:T(256)S(1)} %fusion.109) | copy-start | bytes 3076
  16.0 150.7 %copy-start.55 = (f32[1,256]{1,0:T(1,128)}, f32[1,256]{1,0:T(1,128)S(1)}, u32[]{:S(2)}) copy-start(f32[1,256]{1,0:T(1,128)S(1)} %compare_select_fusion.4) | copy-start | bytes 3076
  16.6 141.3 %copy-start.70 = (f32[48]{0:T(128)S(1)}, f32[48]{0:T(128)}, u32[]{:S(2)}) copy-start(f32[48]{0:T(128)} %param.23) | copy-start | bytes 580
  161.8 10.4 copy-start.64
  164.3 8.0 collective-permute-start
  212.0 129.8 %all-gather.9.cloned.1.call-start = ((), (), s32[]{:S(2)}) async-start(), calls=%async_computation.3 | async-start | bytes 9732096 | tf_op jit(solution)/shard_map/all_gather | solution.py:197
  213.8 213.0 %all-gather.13.cloned.1.call-start = ((), (), s32[]{:S(2)}) async-start(), calls=%async_computation.7 | async-start | bytes 7864320 | tf_op jit(solution)/shard_map/all_gather | solution.py:18
  235.3 10.1 copy-start.30
  256.9 28.3 %copy-start.69 = (s32[1,256]{1,0:T(1,128)S(1)}, s32[1,256]{1,0:T(1,128)}, u32[]{:S(2)}) copy-start(s32[1,256]{1,0:T(1,128)} %param.17) | copy-start | bytes 3076
  292.8 16.9 %copy-start.12 = (f32[256,48,64]{0,2,1:T(8,128)}, f32[256,48,64]{0,2,1:T(8,128)S(1)}, u32[]{:S(2)}) copy-start(f32[256,48,64]{0,2,1:T(8,128)S(1)} %fusion.58) | copy-start | bytes 9437188
  319.3 22.5 %copy-start.31 = (f32[3072]{0:T(1024)S(1)}, f32[3072]{0:T(1024)}, u32[]{:S(2)}) copy-start(f32[3072]{0:T(1024)} %param.26) | copy-start | bytes 36868
  324.8 25.4 %copy-start.51 = (f32[256]{0:T(256)}, f32[256]{0:T(256)S(1)}, u32[]{:S(2)}) copy-start(f32[256]{0:T(256)S(1)} %fusion.110) | copy-start | bytes 3076
  365.7 340.0 %all-reduce.14.cloned.1.call-start = ((), (), s32[]{:S(2)}) async-start(), calls=%async_computation.8 | async-start | bytes 183296 | tf_op jit(solution)/shard_map/psum | solution.py:248
  401.4 19.7 %copy-start.32 = (f32[3072]{0:T(1024)S(1)}, f32[3072]{0:T(1024)}, u32[]{:S(2)}) copy-start(f32[3072]{0:T(1024)} %param.26) | copy-start | bytes 36868
  401.4 19.7 %copy-start.52 = (f32[256]{0:T(256)S(1)}, f32[256]{0:T(256)}, u32[]{:S(2)}) copy-start(f32[256]{0:T(256)} %copy-done.51) | copy-start | bytes 3076
  401.4 19.7 %copy-start.62 = (f32[256]{0:T(256)S(1)}, f32[256]{0:T(256)}, u32[]{:S(2)}) copy-start(f32[256]{0:T(256)} %copy-done.61) | copy-start | bytes 3076
  403.0 16.2 %copy-start.24 = (f32[256,256]{1,0:T(8,128)S(1)}, f32[256,256]{1,0:T(8,128)}, u32[]{:S(2)}) copy-start(f32[256,256]{1,0:T(8,128)} %get-tuple-element.412) | copy-start | bytes 786436
  403.0 18.2 %copy-start.2 = (f32[256,3072]{1,0:T(8,128)S(1)}, f32[256,3072]{1,0:T(8,128)}, u32[]{:S(2)}) copy-start(f32[256,3072]{1,0:T(8,128)} %get-tuple-element.467) | copy-start | bytes 9437188
  503.6 30.8 %copy-start.35 = (f32[3328]{0:T(1024)S(1)}, f32[3328]{0:T(1024)}, u32[]{:S(2)}) copy-start(f32[3328]{0:T(1024)} %get-tuple-element.422) | copy-start | bytes 39940
  503.7 30.8 %copy-start.37 = (f32[3328]{0:T(1024)S(1)}, f32[3328]{0:T(1024)}, u32[]{:S(2)}) copy-start(f32[3328]{0:T(1024)} %get-tuple-element.423) | copy-start | bytes 39940
  503.7 30.8 %copy-start.39 = (f32[3328]{0:T(1024)S(1)}, f32[3328]{0:T(1024)}, u32[]{:S(2)}) copy-start(f32[3328]{0:T(1024)} %get-tuple-element.424) | copy-start | bytes 39940
  503.7 30.8 %copy-start.41 = (f32[3328]{0:T(1024)S(1)}, f32[3328]{0:T(1024)}, u32[]{:S(2)}) copy-start(f32[3328]{0:T(1024)} %get-tuple-element.425) | copy-start | bytes 39940
  546.0 9.3 copy-start.45
  546.0 9.3 copy-start.46
  546.0 10.0 copy-start.18
  546.0 10.0 copy-start.20
  546.0 10.0 copy-start.23
  546.0 10.0 copy-start.25
  546.0 10.0 copy-start.26
  546.0 10.0 copy-start.27
  546.1 10.0 copy-start.56
  546.1 10.0 copy-start.71
  546.1 10.0 copy-start.73
  546.1 10.0 copy-start.75
  546.1 10.7 copy-start.77
  554.0 6.8 collective-permute-start.2
  566.7 12.7 copy-start.3
  566.7 12.7 copy-start.33
  566.7 12.7 copy-start.53
  579.3 341.0 %reduce-scatter.5.cloned.1.call-start = ((), (), s32[]{:S(2)}) async-start(), calls=%async_computation.5 | async-start | bytes 19464192 | tf_op jit(solution)/shard_map/reduce_scatter | solution.py:204
  588.5 701.7 %reduce-scatter.3.cloned.1.call-start = ((), (), s32[]{:S(2)}) async-start(), calls=%async_computation.4 | async-start | bytes 41361408 | tf_op jit(solution)/shard_map/reduce_scatter | solution.py:241
  (40 other events, 213.6 us)
Sparse Core Ops, SparseCore 0:
  11.5 130.6 all-gather.6
  212.1 44.7 all-gather.10
  260.4 81.2 all-gather.8
  365.8 44.9 all-gather.12
  579.5 126.1 all-reduce.13
  712.5 207.7 reduce-scatter.4
  927.3 362.8 reduce-scatter.2
where the time goes:
time: 1310 us
  waiting for transfers between devices  825 us (63%)
  matrix products  166 us (13%)
  other arithmetic  163 us (12%)
  local copies, waits for them, and re-layouts  102 us (8%)
  blocking collectives  19.8 us (2%)
  between operations  16.3 us (1%)
    reduce_scatter x1, waiting for transfers between devices, shards(): lax.psum_scatter(in_term, ('dp', 'seq'), scatter_dimension=0, tiled=True)  370 us
    reduce_scatter x1, waiting for transfers between devices, shards(): lax.psum_scatter(out_term, ('dp', 'seq'), scatter_dimension=0, tiled=True)  215 us
    all_gather x1, waiting for transfers between devices, shards(): in_full = lax.all_gather(in_low, ('dp', 'seq'), axis=0, tiled=True)  126 us
    psum x1, waiting for transfers between devices, shards(): lax.psum((d_norm_gain, d_conv_weight, d_conv_bias, d_step_bias, d_log_rat...  89.9 us
    dot_general x3, matrix products, block_inner(): output = jnp.einsum('hts,shp->thp', weights, x_heads, precision=highest)  53.6 us
    reduce_sum x1, other arithmetic, conv_mixer(): conv_weight[offset] * extended[:, begin_at:begin_at + block, :]  27.5 us
  transfers between devices with their start and end apart: 10, of which 6 were waited for; matrix products, arithmetic and copies ran while one was open for 14% of the time, Pallas kernels for 0%

commit v1 on v0

v1 whole, which is shorter than its diff:
```python
import functools

import jax
import jax.numpy as jnp
from jax import lax
from jax.experimental import pallas as pl
from jax.experimental.pallas import tpu as pltpu
from jax.sharding import PartitionSpec as P

epsilon = 1e-05
highest = lax.Precision.HIGHEST
f32 = jnp.float32
bf16 = jnp.bfloat16
LANES = 128
HALO = 16
NEG = -1e30


def mm(a, b, dims, out=f32):
    return lax.dot_general(a, b, (dims, ((), ())), preferred_element_type=out)


NN = ((1,), (0,))
NT = ((1,), (1,))
TN = ((0,), (0,))


def exact(a, b, dims):
    return lax.dot_general(a, b, (dims, ((), ())), precision=highest, preferred_element_type=f32)


def softplus(v):
    return jnp.maximum(v, 0.0) + jnp.log1p(jnp.exp(-jnp.abs(v)))


def sigmoid(v):
    return 1.0 / (1.0 + jnp.exp(-v))


def lane_iota(shape):
    return lax.broadcasted_iota(jnp.int32, shape, len(shape) - 1)


def spread(columns, first, second, wide):
    rows = columns.shape[0]
    left = jnp.broadcast_to(columns[:, first : first + 1], (rows, LANES))
    right = jnp.broadcast_to(columns[:, second : second + 1], (rows, LANES))
    return jnp.where(wide, left, right)


def step_parts(raw, rate, q):
    row = lax.broadcasted_iota(jnp.int32, (q, q), 0)
    col = lax.broadcasted_iota(jnp.int32, (q, q), 1)
    tri = jnp.where(row >= col, 1.0, 0.0).astype(f32)
    step = softplus(raw)
    decay = -step * rate
    total = exact(tri, decay, NN)
    return step, decay, total, tri, row >= col


def convolve(ext, docs_ext, own, weights, bias, lanes, q, taps):
    running = bias + weights[0:1, lanes] * ext[pl.ds(HALO, q), lanes]
    for lag in range(1, taps):
        same = jnp.where(docs_ext[pl.ds(HALO - lag, q), :] == own, 1.0, 0.0)
        running = running + weights[lag : lag + 1, lanes] * ext[pl.ds(HALO - lag, q), lanes] * same
    return running


def scan_forward(
    q, taps, pairs, head,
    x_ref, small_ref, bct_ref, dcol_ref, drow_ref, w_ref, b_ref, sb_ref, rate_ref, skip_ref,
    y_ref, states_ref,
    state, ext, docs_ext, xs, xt, last_doc,
):
    c = pl.program_id(0)
    n = bct_ref.shape[0] // 2

    @pl.when(c == 0)
    def _():
        state[...] = jnp.zeros_like(state)
        ext[pl.ds(0, HALO), :] = jnp.zeros((HALO, ext.shape[1]), f32)
        docs_ext[pl.ds(0, HALO), :] = jnp.full((HALO, LANES), -1.0, f32)
        last_doc[...] = jnp.full(last_doc.shape, -1.0, f32)

    own = dcol_ref[...]
    ext[pl.ds(HALO, q), :] = x_ref[...].astype(f32)
    docs_ext[pl.ds(HALO, q), :] = own
    step, _, cum, _, causal = step_parts(small_ref[...] + sb_ref[...], rate_ref[...], q)
    step_t = step.T
    cum_t = cum.T
    end = cum[q - 1 : q, :]
    id_in = last_doc[0:1, :]
    final = own[q - 1 : q, :]
    linked = jnp.where(final == id_in, 1.0, 0.0)
    fade = linked * jnp.exp(end)
    entering = jnp.where(own == id_in, 1.0, 0.0) * jnp.exp(cum)
    to_end = jnp.where(own == final, 1.0, 0.0) * jnp.exp(end - cum) * step
    same_doc = jnp.broadcast_to(own[:, 0:1], (q, q)) == jnp.broadcast_to(drow_ref[0:1, :], (q, q))
    hide = jnp.where(jnp.logical_and(causal, same_doc), 0.0, NEG)
    bt = bct_ref[0:n, :]
    ct = bct_ref[n : 2 * n, :]
    scores = mm(ct, bt, TN)
    states_ref[0] = state[...]
    old = state[...].astype(bf16)
    wide = lane_iota((q, LANES)) < head
    wide_row = lane_iota((1, LANES)) < head
    for k in range(pairs):
        lanes = slice(k * LANES, (k + 1) * LANES)
        h0, h1 = 2 * k, 2 * k + 1
        conv = convolve(ext, docs_ext, own, w_ref, b_ref[:, lanes], lanes, q, taps)
        x = conv * sigmoid(conv)
        xd = x * spread(step, h0, h1, wide)
        xt[:, lanes] = (x * spread(to_end, h0, h1, wide)).astype(bf16)
        mats = []
        for h in (h0, h1):
            gap = cum[:, h : h + 1] - cum_t[h : h + 1, :] + hide
            mats.append((jnp.exp(gap) * scores).astype(bf16))
        out = mm(mats[0], jnp.where(wide, xd, 0.0).astype(bf16), NN)
        out = out + mm(mats[1], jnp.where(wide, 0.0, xd).astype(bf16), NN)
        out = out + mm(ct, old[:, lanes], TN) * spread(entering, h0, h1, wide)
        y_ref[:, lanes] = out + skip_ref[:, lanes] * x
    update = mm(bt, xt[...], NN)
    for k in range(pairs):
        lanes = slice(k * LANES, (k + 1) * LANES)
        state[:, lanes] = state[:, lanes] * spread(fade, 2 * k, 2 * k + 1, wide_row) + update[:, lanes]
    ext[pl.ds(0, HALO), :] = ext[pl.ds(q, HALO), :]
    docs_ext[pl.ds(0, HALO), :] = docs_ext[pl.ds(q, HALO), :]
    last_doc[...] = jnp.broadcast_to(final, last_doc.shape)


def scan_backward(
    q, taps, pairs, head, chunks,
    x_ref, xp_ref, small_ref, bct_ref, dcol_ref, dcolp_ref, drow_ref, w_ref, b_ref, sb_ref, rate_ref,
    skip_ref, dy_ref, states_ref,
    dx_ref, dsmall_ref, dbct_ref, dconv_ref, dhead_ref,
    dstate, ext, docs_ext, dcv, docs_after, dye, xt, col_t,
):
    step_at = pl.program_id(0)
    c = chunks - 1 - step_at
    n = bct_ref.shape[0] // 2
    width = x_ref.shape[1]

    @pl.when(step_at == 0)
    def _():
        dstate[...] = jnp.zeros_like(dstate)
        dcv[pl.ds(q, HALO), :] = jnp.zeros((HALO, width), f32)
        docs_after[pl.ds(q, HALO), :] = jnp.full((HALO, LANES), -1.0, f32)
        dconv_ref[...] = jnp.zeros_like(dconv_ref)
        dhead_ref[...] = jnp.zeros_like(dhead_ref)
        col_t[...] = jnp.zeros_like(col_t)

    first = c == 0
    own = dcol_ref[...]
    before = jnp.where(first, -1.0, dcolp_ref[...])
    ext[pl.ds(0, HALO), :] = xp_ref[...].astype(f32)
    ext[pl.ds(HALO, q), :] = x_ref[...].astype(f32)
    docs_ext[pl.ds(0, HALO), :] = before
    docs_ext[pl.ds(HALO, q), :] = own
    docs_after[pl.ds(0, q), :] = own
    raw = small_ref[...] + sb_ref[...]
    rate = rate_ref[...]
    step, decay, cum, tri, causal = step_parts(raw, rate, q)
    step_t = step.T
    cum_t = cum.T
    end = cum[q - 1 : q, :]
    id_in = before[HALO - 1 : HALO, :]
    final = own[q - 1 : q, :]
    linked = jnp.where(final == id_in, 1.0, 0.0)
    fade = linked * jnp.exp(end)
    entering = jnp.where(own == id_in, 1.0, 0.0) * jnp.exp(cum)
    tail = jnp.where(own == final, 1.0, 0.0) * jnp.exp(end - cum)
    to_end = tail * step
    same_doc = jnp.broadcast_to(own[:, 0:1], (q, q)) == jnp.broadcast_to(drow_ref[0:1, :], (q, q))
    hide = jnp.where(jnp.logical_and(causal, same_doc), 0.0, NEG)
    bt = bct_ref[0:n, :]
    ct = bct_ref[n : 2 * n, :]
    scores = mm(ct, bt, TN)
    old = states_ref[0].astype(bf16)
    after = dstate[...].astype(bf16)
    wide = lane_iota((q, LANES)) < head
    wide_row = lane_iota((1, LANES)) < head
    lane = lane_iota((q, LANES))
    d_scores = jnp.zeros((q, q), f32)
    rows = jnp.zeros((q, LANES), f32)
    d_enter = jnp.zeros((q, LANES), f32)
    d_toend = jnp.zeros((q, LANES), f32)
    d_fade = jnp.zeros((8, LANES), f32)
    part = lax.broadcasted_iota(jnp.int32, (LANES, LANES), 0) // head
    to = lane_iota((LANES, LANES))
    for k in range(pairs):
        lanes = slice(k * LANES, (k + 1) * LANES)
        h0, h1 = 2 * k, 2 * k + 1
        pick = jnp.where(part + 2 * k == to, 1.0, 0.0)
        conv = convolve(ext, docs_ext, own, w_ref, b_ref[:, lanes], lanes, q, taps)
        sig = sigmoid(conv)
        x = conv * sig
        xb = x.astype(bf16)
        dy = dy_ref[:, lanes]
        halves = (jnp.where(wide, dy, 0.0).astype(bf16), jnp.where(wide, 0.0, dy).astype(bf16))
        dxd = jnp.zeros((q, LANES), f32)
        for h, half in ((h0, halves[0]), (h1, halves[1])):
            inner = mm(half, xb, NT)
            keep = jnp.exp(cum[:, h : h + 1] - cum_t[h : h + 1, :] + hide)
            grown = keep * inner
            mat = keep * scores
            dt = step_t[h : h + 1, :]
            g = grown * scores
            d_scores = d_scores + grown * dt
            rows = jnp.where(lane == h, jnp.sum(g * dt, axis=1, keepdims=True), rows)
            col_t[h : h + 1, :] = jnp.sum(g, axis=0, keepdims=True)
            dxd = dxd + mm(mat.astype(bf16), half, TN)
        v = mm(bt, after[:, lanes], TN)
        u = mm(ct, old[:, lanes], TN)
        enter_k = spread(entering, h0, h1, wide)
        end_k = spread(to_end, h0, h1, wide)
        d_enter = d_enter + exact(dy * u, pick, NN)
        d_toend = d_toend + exact(x * v, pick, NN)
        hh = jnp.sum(dstate[:, lanes] * states_ref[0, :, lanes], axis=0, keepdims=True)
        d_fade = d_fade + exact(jnp.broadcast_to(hh, (8, LANES)), pick, NN)
        dye[:, lanes] = (dy * enter_k).astype(bf16)
        xt[:, lanes] = (x * end_k).astype(bf16)
        dx = dxd * spread(step, h0, h1, wide) + end_k * v + skip_ref[:, lanes] * dy
        dconv = dx * (sig * (1.0 + conv * (1.0 - sig)))
        dcv[pl.ds(0, q), lanes] = dconv
        sums = [jnp.sum(dconv * ext[pl.ds(HALO, q), lanes], axis=0, keepdims=True)]
        dxin = w_ref[0:1, lanes] * dconv
        for lag in range(1, taps):
            same = jnp.where(docs_ext[pl.ds(HALO - lag, q), :] == own, 1.0, 0.0)
            sums.append(jnp.sum(dconv * same * ext[pl.ds(HALO - lag, q), lanes], axis=0, keepdims=True))
            follow = jnp.where(docs_after[pl.ds(lag, q), :] == own, 1.0, 0.0)
            dxin = dxin + w_ref[lag : lag + 1, lanes] * dcv[pl.ds(lag, q), lanes] * follow
        sums.append(jnp.sum(dconv, axis=0, keepdims=True))
        sums.append(jnp.sum(dy * x, axis=0, keepdims=True))
        dx_ref[:, lanes] = dxin.astype(bf16)
        for i, s in enumerate(sums):
            dconv_ref[i : i + 1, lanes] = dconv_ref[i : i + 1, lanes] + s
    dsb = d_scores.astype(bf16)
    dbct_ref[0:n, :] = mm(ct, dsb, NN) + mm(after, xt[...], NT)
    dbct_ref[n : 2 * n, :] = mm(bt, dsb, NT) + mm(old, dye[...], NT)
    new = mm(ct, dye[...], NN)
    for k in range(pairs):
        lanes = slice(k * LANES, (k + 1) * LANES)
        dstate[:, lanes] = dstate[:, lanes] * spread(fade, 2 * k, 2 * k + 1, wide_row) + new[:, lanes]
    cols = col_t[...].T
    pulled = d_toend * to_end
    at_end = jnp.sum(pulled, axis=0, keepdims=True) + fade * d_fade[0:1, :]
    d_cum = rows - step * cols + d_enter * entering - pulled
    last_row = lax.broadcasted_iota(jnp.int32, (q, LANES), 0) == q - 1
    d_cum = d_cum + jnp.where(last_row, at_end, 0.0)
    d_decay = exact(tri, d_cum, TN)
    d_step = cols + d_toend * tail - rate * d_decay
    d_raw = d_step * sigmoid(raw)
    dsmall_ref[...] = d_raw
    dhead_ref[0:1, :] = dhead_ref[0:1, :] + jnp.sum(d_raw, axis=0, keepdims=True)
    dhead_ref[1:2, :] = dhead_ref[1:2, :] + jnp.sum(d_decay * decay, axis=0, keepdims=True)
    dcv[pl.ds(q, HALO), :] = dcv[pl.ds(0, HALO), :]
    docs_after[pl.ds(q, HALO), :] = docs_after[pl.ds(0, HALO), :]


def whole(array):
    return pl.BlockSpec(array.shape, lambda c: (0,) * array.ndim)


def run_forward(q, x_in, small, bct, dcol, drow, conv_w, conv_b, sb, rate, skip, head):
    tokens, width = x_in.shape
    n = bct.shape[0] // 2
    chunks = tokens // q
    pairs = width // LANES
    taps = conv_w.shape[0]
    return pl.pallas_call(
        functools.partial(scan_forward, q, taps, pairs, head),
        grid=(chunks,),
        in_specs=[
            pl.BlockSpec((q, width), lambda c: (c, 0)),
            pl.BlockSpec((q, LANES), lambda c: (c, 0)),
            pl.BlockSpec((2 * n, q), lambda c: (0, c)),
            pl.BlockSpec((q, LANES), lambda c: (c, 0)),
            pl.BlockSpec((8, q), lambda c: (0, c)),
            whole(conv_w), whole(conv_b), whole(sb), whole(rate), whole(skip),
        ],
        out_specs=[
            pl.BlockSpec((q, width), lambda c: (c, 0)),
            pl.BlockSpec((1, n, width), lambda c: (c, 0, 0)),
        ],
        out_shape=[
            jax.ShapeDtypeStruct((tokens, width), f32),
            jax.ShapeDtypeStruct((chunks, n, width), f32),
        ],
        scratch_shapes=[
            pltpu.VMEM((n, width), f32),
            pltpu.VMEM((HALO + q, width), f32),
            pltpu.VMEM((HALO + q, LANES), f32),
            pltpu.VMEM((8, LANES), f32),
            pltpu.VMEM((q, width), bf16),
            pltpu.VMEM((8, LANES), f32),
        ],
        name="scan_forward",
    )(x_in, small, bct, dcol, drow, conv_w, conv_b, sb, rate, skip)


def run_backward(q, x_in, small, bct, dcol, drow, conv_w, conv_b, sb, rate, skip, dy, states, head):
    tokens, width = x_in.shape
    n = bct.shape[0] // 2
    chunks = tokens // q
    pairs = width // LANES
    taps = conv_w.shape[0]
    per = q // HALO

    def at(c):
        return chunks - 1 - c

    def prior(c):
        return jnp.maximum((chunks - 1 - c) * per - 1, 0)

    return pl.pallas_call(
        functools.partial(scan_backward, q, taps, pairs, head, chunks),
        grid=(chunks,),
        in_specs=[
            pl.BlockSpec((q, width), lambda c: (at(c), 0)),
            pl.BlockSpec((HALO, width), lambda c: (prior(c), 0)),
            pl.BlockSpec((q, LANES), lambda c: (at(c), 0)),
            pl.BlockSpec((2 * n, q), lambda c: (0, at(c))),
            pl.BlockSpec((q, LANES), lambda c: (at(c), 0)),
            pl.BlockSpec((HALO, LANES), lambda c: (prior(c), 0)),
            pl.BlockSpec((8, q), lambda c: (0, at(c))),
            whole(conv_w), whole(conv_b), whole(sb), whole(rate), whole(skip),
            pl.BlockSpec((q, width), lambda c: (at(c), 0)),
            pl.BlockSpec((1, n, width), lambda c: (at(c), 0, 0)),
        ],
        out_specs=[
            pl.BlockSpec((q, width), lambda c: (at(c), 0)),
            pl.BlockSpec((q, LANES), lambda c: (at(c), 0)),
            pl.BlockSpec((2 * n, q), lambda c: (0, at(c))),
            pl.BlockSpec((8, width), lambda c: (0, 0)),
            pl.BlockSpec((8, LANES), lambda c: (0, 0)),
        ],
        out_shape=[
            jax.ShapeDtypeStruct((tokens, width), bf16),
            jax.ShapeDtypeStruct((tokens, LANES), f32),
            jax.ShapeDtypeStruct((2 * n, tokens), f32),
            jax.ShapeDtypeStruct((8, width), f32),
            jax.ShapeDtypeStruct((8, LANES), f32),
        ],
        scratch_shapes=[
            pltpu.VMEM((n, width), f32),
            pltpu.VMEM((HALO + q, width), f32),
            pltpu.VMEM((HALO + q, LANES), f32),
            pltpu.VMEM((q + HALO, width), f32),
            pltpu.VMEM((q + HALO, LANES), f32),
            pltpu.VMEM((q, width), bf16),
            pltpu.VMEM((q, width), bf16),
            pltpu.VMEM((LANES, q), f32),
        ],
        name="scan_backward",
    )(x_in, x_in, small, bct, dcol, dcol, drow, conv_w, conv_b, sb, rate, skip, dy, states)


def swapped(block, bit):
    size = lax.axis_size("seq")
    return lax.ppermute(block, "seq", [(i, i ^ bit) for i in range(size)])


def bits_of(size):
    bits, bit = [], 1
    while bit < size:
        bits.append(bit)
        bit *= 2
    return bits


def gathered(block):
    index = lax.axis_index("seq")
    for bit in bits_of(lax.axis_size("seq")):
        other = swapped(block, bit)
        upper = (index & bit) != 0
        block = jnp.where(
            upper, jnp.concatenate([other, block], axis=0), jnp.concatenate([block, other], axis=0)
        )
    return block


def scattered(parts):
    index = lax.axis_index("seq")
    size = lax.axis_size("seq")
    rest = parts.shape[1:]
    lead = parts.shape[0]
    held = parts.reshape((size, lead // size) + rest)
    for bit in bits_of(size):
        half = held.reshape((held.shape[0] // 2, 2) + held.shape[1:])
        upper = (index & bit) != 0
        mine = jnp.where(upper, half[:, 1], half[:, 0])
        theirs = jnp.where(upper, half[:, 0], half[:, 1]).astype(bf16)
        held = mine.astype(f32) + swapped(theirs, bit).astype(f32)
    return held[0]


def padded(rows, width):
    return jnp.pad(rows, ((0, 0), (0, width - rows.shape[1])))


def shards(
    hidden, segments, cotangent, norm_gain, in_weight, conv_weight, conv_bias, step_bias, log_rate,
    skip_gain, gate_gain, out_weight,
):
    n_seqs, block, n_width = hidden.shape
    size = lax.axis_size("seq")
    groups = lax.axis_size("dp")
    index = lax.axis_index("seq")
    tokens = size * block
    n_inner = gate_gain.shape[0]
    n_heads = step_bias.shape[0]
    n_taps = conv_weight.shape[0]
    n_mixed = conv_bias.shape[0]
    n_state = (n_mixed - n_inner) // 2
    head = n_inner // n_heads
    own_inner = n_inner // size
    own_heads = n_heads // size
    own_bc = 2 * n_state // size
    q = min(128, block)
    in_rows = in_weight.shape[0]

    in_low = in_weight.astype(bf16)
    z_cols = in_low[:, :n_inner].reshape(in_rows, size, own_inner)
    x_cols = in_low[:, n_inner : 2 * n_inner].reshape(in_rows, size, own_inner)
    bc_cols = in_low[:, 2 * n_inner : n_inner + n_mixed].reshape(in_rows, size, own_bc)
    dt_cols = in_low[:, n_inner + n_mixed :].reshape(in_rows, size, own_heads)
    gap = jnp.zeros((in_rows, size, LANES - own_heads - own_bc), bf16)
    laid = jnp.concatenate([x_cols, dt_cols, gap, bc_cols, z_cols], axis=2).transpose(1, 0, 2)
    mine = lax.all_to_all(laid, "seq", 0, 0, tiled=True)
    mine = mine.reshape(size * in_rows, -1)
    n_first = own_inner + LANES
    w_first = lax.all_gather(mine[:, :n_first], "dp", axis=0, tiled=True)
    w_z = lax.all_gather(mine[:, n_first:], "dp", axis=0, tiled=True)
    order = [(f, (f % groups) * size + f // groups) for f in range(groups * size)]
    back = [(b, a) for a, b in order]
    out_moved = lax.ppermute(out_weight.astype(bf16), ("dp", "seq"), order)
    w_out = lax.all_gather(out_moved, "dp", axis=0, tiled=True)

    flat = hidden.reshape(block, n_width).astype(f32)
    inv = lax.rsqrt(jnp.mean(flat * flat, axis=-1, keepdims=True) + epsilon)
    unit = flat * inv
    normed = gathered((unit * norm_gain).astype(bf16))
    cot_own = cotangent.reshape(block, n_width)
    cot = gathered(cot_own)
    docs = lax.all_gather(segments.reshape(block), "seq", axis=0, tiled=True).astype(f32)
    dcol = jnp.broadcast_to(docs[:, None], (tokens, LANES))
    drow = jnp.broadcast_to(docs[None, :], (8, tokens))

    def own_part(vector, parts):
        return lax.dynamic_slice_in_dim(vector, index * parts, parts, vector.ndim - 1)

    w_x, w_small = w_first[:, :own_inner], w_first[:, own_inner:]
    small = mm(normed, w_small, NN)
    x_in = mm(normed, w_x, NN).astype(bf16)
    z = mm(normed, w_z, NN)
    conv_x = own_part(conv_weight[:, :n_inner], own_inner)
    bias_x = own_part(conv_bias[None, :n_inner], own_inner)
    conv_bc = own_part(conv_weight[:, n_inner:], own_bc)
    bias_bc = own_part(conv_bias[None, n_inner:], own_bc)
    sb = padded(own_part(step_bias[None], own_heads), LANES)
    rate = padded(jnp.exp(own_part(log_rate[None], own_heads)), LANES)
    skip = jnp.repeat(own_part(skip_gain[None], own_heads), head, axis=1)
    gain = own_part(gate_gain[None], own_inner)

    head_lanes = jnp.arange(LANES) < own_heads
    bc_in = small[:, LANES - own_bc :].astype(bf16).astype(f32)
    small_dt = jnp.where(head_lanes, small, 0.0)

    def earlier(rows, lag):
        return jnp.pad(rows, ((lag, 0), (0, 0)))[:tokens]

    def later(rows, lag):
        return jnp.pad(rows, ((0, lag), (0, 0)))[lag:]

    same = [None] + [
        jnp.where(jnp.pad(docs, (lag, 0), constant_values=-1.0)[:tokens] == docs, 1.0, 0.0)[:, None]
        for lag in range(1, n_taps)
    ]
    bc_conv = bias_bc + conv_bc[0:1] * bc_in
    for lag in range(1, n_taps):
        bc_conv = bc_conv + conv_bc[lag : lag + 1] * earlier(bc_in, lag) * same[lag]
    bc_sig = jax.nn.sigmoid(bc_conv)
    bct = lax.all_gather((bc_conv * bc_sig).astype(bf16).T, "seq", axis=0, tiled=True)

    y, states = run_forward(
        q, x_in, small_dt, bct, dcol, drow, conv_x, bias_x, sb, rate, skip, head
    )

    d_gn = mm(cot, w_out, NT)
    z_sig = jax.nn.sigmoid(z)
    z_act = z * z_sig
    gated = y * z_act
    scaled = d_gn * gain
    both = jnp.stack([jnp.sum(gated * gated, axis=1), jnp.sum(scaled * gated, axis=1)])
    both = lax.psum(both, "seq")
    g_inv = lax.rsqrt(both[0] / n_inner + epsilon)[:, None]
    g_dot = both[1][:, None] / n_inner
    gate_low = (gated * g_inv * gain).astype(bf16)
    d_gated = g_inv * scaled - gated * (g_inv * g_inv * g_inv * g_dot)
    d_gain = jnp.sum(d_gn * gated * g_inv, axis=0)
    d_z = (d_gated * y * (z_sig * (1.0 + z * (1.0 - z_sig)))).astype(bf16)
    d_y = d_gated * z_act

    branch = scattered(mm(gate_low, w_out, NN).astype(bf16))
    result = (flat + branch).reshape(n_seqs, block, n_width).astype(bf16)
    out_term = mm(gate_low, cot, TN).astype(bf16)
    z_term = mm(normed, d_z, TN).astype(bf16)
    out_part = lax.psum_scatter(out_term, "dp", scatter_dimension=0, tiled=True)
    z_part = lax.psum_scatter(z_term, "dp", scatter_dimension=0, tiled=True)
    d_out_weight = lax.ppermute(out_part, ("dp", "seq"), back).astype(f32)

    d_x, d_dt, d_bct, d_conv_x, d_heads = run_backward(
        q, x_in, small_dt, bct, dcol, drow, conv_x, bias_x, sb, rate, skip, d_y, states, head
    )
    d_bc = scattered(d_bct).T
    d_bcc = d_bc * (bc_sig * (1.0 + bc_conv * (1.0 - bc_sig)))
    d_bc_in = conv_bc[0:1] * d_bcc
    w_sums = [jnp.sum(d_bcc * bc_in, axis=0)]
    for lag in range(1, n_taps):
        held = d_bcc * same[lag]
        d_bc_in = d_bc_in + conv_bc[lag : lag + 1] * later(held, lag)
        w_sums.append(jnp.sum(held * earlier(bc_in, lag), axis=0))
    w_sums.append(jnp.sum(d_bcc, axis=0))
    d_small = jnp.concatenate([d_dt[:, : LANES - own_bc], d_bc_in], axis=1).astype(bf16)
    d_first = jnp.concatenate([d_x, d_small], axis=1)
    first_term = mm(normed, d_first, TN).astype(bf16)
    first_part = lax.psum_scatter(first_term, "dp", scatter_dimension=0, tiled=True)
    d_normed = mm(d_first, w_first, NT) + mm(d_z, w_z, NT)
    d_norm = scattered(d_normed.astype(bf16))

    term = jnp.concatenate([first_part, z_part], axis=1).reshape(size, in_rows, -1)
    moved = lax.all_to_all(term, "seq", 0, 0, tiled=True).transpose(1, 0, 2).astype(f32)
    d_in_weight = jnp.concatenate(
        [
            moved[:, :, n_first:].reshape(in_rows, n_inner),
            moved[:, :, :own_inner].reshape(in_rows, n_inner),
            moved[:, :, n_first - own_bc : n_first].reshape(in_rows, 2 * n_state),
            moved[:, :, own_inner : own_inner + own_heads].reshape(in_rows, n_heads),
        ],
        axis=1,
    )

    d_norm_gain = jnp.sum(d_norm * unit, axis=0)
    lifted = d_norm * norm_gain
    d_flat = inv * lifted - flat * (
        inv * inv * inv * jnp.mean(lifted * flat, axis=-1, keepdims=True)
    )
    d_hidden = (cot_own.astype(f32) + d_flat).reshape(n_seqs, block, n_width)

    d_skip = jnp.sum(d_conv_x[n_taps + 1].reshape(own_heads, head), axis=1)
    packed = jnp.concatenate(
        [
            d_conv_x[: n_taps + 1].reshape(-1),
            jnp.stack(w_sums).reshape(-1),
            d_gain,
            d_heads[0, :own_heads],
            d_heads[1, :own_heads],
            d_skip,
            d_norm_gain,
        ]
    )
    packed = jnp.sum(lax.all_gather(packed, "dp", axis=0), axis=0)
    packed = lax.all_gather(packed, "seq", axis=0)
    at = 0

    def take(count):
        nonlocal at
        at += count
        return packed[:, at - count : at]

    got_x = take((n_taps + 1) * own_inner).reshape(size, n_taps + 1, own_inner)
    got_bc = take((n_taps + 1) * own_bc).reshape(size, n_taps + 1, own_bc)
    got_x = got_x.transpose(1, 0, 2).reshape(n_taps + 1, n_inner)
    got_bc = got_bc.transpose(1, 0, 2).reshape(n_taps + 1, 2 * n_state)
    conv_all = jnp.concatenate([got_x, got_bc], axis=1)
    d_gate_gain = take(own_inner).reshape(n_inner)
    d_step_bias = take(own_heads).reshape(n_heads)
    d_log_rate = take(own_heads).reshape(n_heads)
    d_skip_gain = take(own_heads).reshape(n_heads)
    d_norm_all = jnp.sum(take(n_width), axis=0)
    return (
        result,
        d_hidden,
        d_norm_all,
        d_in_weight,
        conv_all[:n_taps],
        conv_all[n_taps],
        d_step_bias,
        d_log_rate,
        d_skip_gain,
        d_gate_gain,
        d_out_weight,
    )


def solution(mesh):
    tokens = P("dp", "seq", None)
    rows = P(("dp", "seq"), None)
    return jax.shard_map(
        shards,
        mesh=mesh,
        in_specs=(tokens, P("dp", "seq"), tokens, P(), rows, P(), P(), P(), P(), P(), P(), rows),
        out_specs=(tokens, tokens, P(), rows, P(), P(), P(), P(), P(), P(), rows),
        check_vma=False,
    )
```

time: 1310 us -> 664 us (0.51)
  waiting for transfers between devices: 825 us -> 408 us
  other arithmetic: 163 us -> 33.8 us
  matrix products: 166 us -> 65.6 us
  local copies, waits for them, and re-layouts: 102 us -> 21.6 us
  Pallas kernels: 0 us -> 44.1 us
  starting transfers between devices: 5.68 us -> 35 us
  blocking collectives: 19.8 us -> 33.1 us
    reduce_scatter x2 -> x3, waiting for transfers between devices: 584 us -> 187 us  [the longest x1 74.7 us: shards(): lax.psum_scatter(first_term, 'dp', scatter_dimension=0, tiled=True)]
    dot_general x18 -> x10, matrix products: 166 us -> 65.6 us  [mm(): return lax.dot_general(a, b, (dims, ((), ())), preferred_element_type=out)]
    psum x1 -> x0, waiting for transfers between devices: 89.9 us -> none  [shards(): lax.psum((d_norm_gain, d_conv_weight, d_conv_bias, d_step_bias, d_log_rat...]
    ppermute x3 -> x12, waiting for transfers between devices: 0.01 us -> 74.3 us  [the longest x10 43.6 us: swapped(): return lax.ppermute(block, 'seq', [(i, i ^ bit) for i in range(size)])]
    all_gather x4 -> x3, waiting for transfers between devices: 151 us -> 77.7 us  [the longest x1 49.3 us: shards(): w_first = lax.all_gather(mine[:, :n_first], 'dp', axis=0, tiled=True)]
    unnamed x7 -> x10, waiting for transfers between devices: 0.11 us -> 68.7 us
    pallas_call x0 -> x2, Pallas kernels: none -> 44.1 us  [the longest x1 30.6 us: run_backward(): pl.pallas_call(functools.partial(scan_backward, q, taps, pairs, head, chu...]
    reduce_sum x9 -> x7, other arithmetic: 46 us -> 6.02 us  [the longest x1 3.09 us: shards(): d_norm_gain = jnp.sum(d_norm * unit, axis=0)]
  transfers between devices with their start and end apart: 10 -> 21, of which waited for: 6 -> 15; matrix products, arithmetic and copies ran while one was open for 14% -> 11% of each run, Pallas kernels for 0% -> 2%
where the time goes in v1:
time: 664 us; the launch traced here: 657 us
  waiting for transfers between devices  408 us (61%)
  matrix products  65.6 us (10%)
  Pallas kernels  44.1 us (7%)
  starting transfers between devices  35 us (5%)
  other arithmetic  33.8 us (5%)
  blocking collectives  33.1 us (5%)
  local copies, waits for them, and re-layouts  21.6 us (3%)
  between operations  16.5 us (2%)
    reduce_scatter x1, waiting for transfers between devices, shards(): lax.psum_scatter(first_term, 'dp', scatter_dimension=0, tiled=True)  74.7 us
    unnamed x10, waiting for transfers between devices  68.7 us
    dot_general x10, matrix products, mm(): return lax.dot_general(a, b, (dims, ((), ())), preferred_element_type=out)  65.6 us
    reduce_scatter x1, waiting for transfers between devices, shards(): out_part = lax.psum_scatter(out_term, 'dp', scatter_dimension=0, tiled=True)  62.5 us
    reduce_scatter x1, waiting for transfers between devices, shards(): z_part = lax.psum_scatter(z_term, 'dp', scatter_dimension=0, tiled=True)  49.8 us
    all_gather x1, waiting for transfers between devices, shards(): w_first = lax.all_gather(mine[:, :n_first], 'dp', axis=0, tiled=True)  49.3 us
    ppermute x10, waiting for transfers between devices, swapped(): return lax.ppermute(block, 'seq', [(i, i ^ bit) for i in range(size)])  43.6 us
    pallas_call x1, Pallas kernels, run_backward(): pl.pallas_call(functools.partial(scan_backward, q, taps, pairs, head, chu...  30.6 us
  transfers between devices with their start and end apart: 21, of which 15 were waited for; matrix products, arithmetic and copies ran while one was open for 11% of the time, Pallas kernels for 2%

profile of v1, /device:TPU:2, one launch (start us, length us, event | category | flops | bytes accessed | tf_op | source)
XLA Modules:
  0.0 657.4 jit_solution(9753306167867401069)
XLA Ops:
  7.2 1.4 convert_element_type.172
  10.2 12.6 %all_to_all.10 = bf16[4,48,1664]{2,1,0:T(8,128)(2,1)S(1)} all-to-all(bf16[4,48,1664]{2,1,0:T(8,128)(2,1)S(1)} %copy.115), channel_id=1, replica_groups=mesh['dp'=8,'seq'=4] {'seq'}, dimensions={0} | all-to-all | bytes 1277952 | tf_op jit(solution)/shard_map/all_to_all | solution.py:429
  25.2 2.3 collective-permute-done
  27.4 1.8 maximum_select_fusion.2
  29.6 4.5 collective-permute-start.4
  34.1 13.5 %collective-permute-done.4 = bf16[96,1536]{1,0:T(8,128)(2,1)S(1)} collective-permute-done((bf16[96,1536]{1,0:T(8,128)(2,1)S(1)}, bf16[96,1536]{1,0:T(8,128)(2,1)S(1)}, u32[]{:S(2)}, u32[]{:S(2)}) %collective-permute-start.4) | collective-permute-done | bytes 294944 | tf_op jit(solution)/shard_map/ppermute | solution.py:436
  48.4 15.3 %collective-permute-start.2 = (bf16[256,1536]{1,0:T(8,128)(2,1)S(1)}, bf16[256,1536]{1,0:T(8,128)(2,1)S(1)}, u32[]{:S(2)}, u32[]{:S(2)}) collective-permute-start(bf16[256,1536]{1,0:T(8,128)(2,1)S(1)} %bitcast.173), channel_id=1, source_target_pairs={{0,1},{1,0},{2,3},{3,2},{4,5},{5,4},{6,7},{7,6},{8,9},{9,8},{10,11... | collective-permute-start | bytes 2359304 | tf_op jit(solution)/shard_map/ppermute | solution.py:360
  63.7 6.4 all-gather
  75.0 3.4 collective-permute-start.3
  78.4 12.0 %all-gather.9.cloned.1.call-done = bf16[1536,768]{1,0:T(8,128)(2,1)} async-done(((bf16[192,768]{1,0:T(8,128)(2,1)}), bf16[1536,768]{1,0:T(8,128)(2,1)}) %all-gather.9.cloned.1.call-update) | async-done | bytes 2359312 | tf_op jit(solution)/shard_map/all_gather | solution.py:433
  90.4 8.0 %fusion.56 = f32[1024,768]{1,0:T(8,128)} fusion(bf16[1536,768]{1,0:T(8,128)(2,1)} %all-gather.9.cloned.1.call-done, bf16[512,1536]{1,0:T(8,128)(2,1)} %maximum_select_fusion.2, bf16[512,1536]{1,0:T(8,128)(2,1)} %collective-permute-done.1, pred[]{:T(512)S(6)} %ne.4), kind=kOutput, calls=%fused_computation.143 | convolution fusion | flops 2430074880 | bytes 8650753 | tf_op jit(solution)/shard_map/dot_general | solution.py:20
  98.4 49.3 %all-gather.7.cloned.1.call-done = bf16[1536,896]{1,0:T(8,128)(2,1)} async-done(((bf16[192,896]{1,0:T(8,128)(2,1)}), bf16[1536,896]{1,0:T(8,128)(2,1)}) %all-gather.7.cloned.1.call-update) | async-done | bytes 2752528 | tf_op jit(solution)/shard_map/all_gather | solution.py:432
  147.8 4.2 fusion.27
  153.2 8.1 %all_gather.29.bct_ref = bf16[256,1024]{1,0:T(8,128)(2,1)} all-gather(bf16[64,1024]{1,0:T(8,128)(2,1)S(1)} %get-tuple-element.40), channel_id=1, replica_groups=mesh['dp'=8,'seq'=4] {'seq'}, dimensions={0}, use_global_device_ids=true | all-gather | bytes 655360 | tf_op jit(solution)/shard_map/all_gather | solution.py:483
  162.2 7.3 %fusion.10.x_ref.xp_ref = bf16[1024,768]{1,0:T(8,128)(2,1)} fusion(bf16[1536,896]{1,0:T(8,128)(2,1)} %all-gather.7.cloned.1.call-done, bf16[512,1536]{1,0:T(8,128)(2,1)} %maximum_select_fusion.2, bf16[512,1536]{1,0:T(8,128)(2,1)} %collective-permute-done.1, pred[]{:T(512)S(6)} %ne.4), kind=kOutput, calls=%fused_computation.30 | convolution fusion | flops 2430861312 | bytes 7077889 | tf_op jit(solution)/shard_map/dot_general | solution.py:20
  171.1 13.4 %scan_forward.1 = (f32[1024,768]{1,0:T(8,128)}, f32[8,128,768]{2,1,0:T(8,128)}) custom-call(bf16[1024,768]{1,0:T(8,128)(2,1)} %fusion.10.x_ref.xp_ref, f32[1024,128]{1,0:T(8,128)} %broadcast_select_fusion.small_ref, bf16[256,1024]{1,0:T(8,128)(2,1)} %all_gather.29.bct_ref, f32[1024,128]{1,0:T(8,128)} %broadcast_in_dim.59.dcol_ref.dcolp_ref, ...), custom_call_target="tpu_custom_call" | custom-call | tf_op jit(solution)/shard_map/scan_forward/pallas_call | solution.py:270
  184.6 16.4 %all-gather.11.cloned.1.call-done = bf16[768,1536]{1,0:T(8,128)(2,1)} async-done(((bf16[96,1536]{1,0:T(8,128)(2,1)}), bf16[768,1536]{1,0:T(8,128)(2,1)}) %all-gather.11.cloned.1.call-update) | async-done | bytes 2359312 | tf_op jit(solution)/shard_map/all_gather | solution.py:437
  201.0 10.2 %multiply_reduce_fusion.2 = (f32[1024]{0:T(1024)S(1)}, f32[1024]{0:T(1024)S(1)}, f32[1024,768]{1,0:T(8,128)S(1)}, f32[1024,768]{1,0:T(8,128)}) fusion(f32[768]{0:T(1024)S(1)} %dynamic-slice.23, f32[1024,768]{1,0:T(8,128)} %get-tuple-element.18, f32[1024,768]{1,0:T(8,128)} %fusion.56, bf16[768,1536]{1,0:T(8,128)(2,1)} %all-gather.11.cloned.1.call-done, ...), kind=kOutput, calls=%fused_computation.16 | convolution fusion | flops 2437937152 | bytes 18099200 | tf_op jit(solution)/shard_map/dot_general | solution.py:20
  211.1 5.9 psum.7
  217.1 6.3 multiply_convert_fusion
  223.4 30.6 %scan_backward.1 = (bf16[1024,768]{1,0:T(8,128)(2,1)}, f32[1024,128]{1,0:T(8,128)}, f32[256,1024]{1,0:T(8,128)}, f32[8,768]{1,0:T(8,128)}, f32[8,128]{1,0:T(8,128)}) custom-call(bf16[1024,768]{1,0:T(8,128)(2,1)} %fusion.10.x_ref.xp_ref, bf16[1024,768]{1,0:T(8,128)(2,1)} %fusion.10.x_ref.xp_ref, f32[1024,128]{1,0:T(8,128)} %broadcast_select_fusion.small_ref, ...), custom_call_target="tpu_custom_call" | custom-call | tf_op jit(solution)/shard_map/scan_backward/pallas_call | solution.py:315
  254.1 1.3 fusion.36
  255.5 1.5 collective-permute-done.7
  258.4 1.8 collective-permute-start.8
  260.2 3.8 collective-permute-done.8
  264.4 1.4 fusion.57
  266.0 5.8 fusion.23
  271.9 3.0 add_convert_fusion
  275.1 3.4 collective-permute-done.9
  280.1 1.7 collective-permute-start.10
  284.2 15.8 %collective-permute-done.10 = bf16[1,256,1536]{2,1,0:T(8,128)(2,1)} collective-permute-done((bf16[1,256,1536]{2,1,0:T(8,128)(2,1)}, bf16[1,256,1536]{2,1,0:T(8,128)(2,1)}, u32[]{:S(2)}, u32[]{:S(2)}) %collective-permute-start.10) | collective-permute-done | bytes 786464 | tf_op jit(solution)/shard_map/ppermute | solution.py:360
  300.0 3.1 fusion.14
  306.0 68.6 %all-reduce.16.cloned.1.call-done = f32[52000]{0:T(1024)} async-done(((f32[52000]{0:T(1024)}), f32[52000]{0:T(1024)}) %all-reduce.16.cloned.1.call-update) | async-done | bytes 208016
  377.0 7.6 %convolution_convert_fusion.3 = bf16[1536,768]{1,0:T(8,128)(2,1)} fusion(bf16[1024,768]{1,0:T(8,128)(2,1)} %get-tuple-element.42, bf16[512,1536]{1,0:T(8,128)(2,1)} %maximum_select_fusion.2, bf16[512,1536]{1,0:T(8,128)(2,1)} %collective-permute-done.1, pred[]{:T(512)S(6)} %ne.4), kind=kOutput, calls=%fused_computation.4 | convolution fusion | flops 2431254528 | bytes 7077889 | tf_op jit(solution)/shard_map/dot_general | solution.py:20
  384.6 8.0 %convolution_convert_fusion.1 = bf16[1536,896]{1,0:T(8,128)(2,1)} fusion(bf16[1024,64]{1,0:T(8,128)(2,1)S(1)} %copy.123, bf16[1024,64]{1,0:T(8,128)(2,1)S(1)} %copy-done.17, bf16[1024,768]{1,0:T(8,128)(2,1)S(1)} %copy-done.25, bf16[512,1536]{1,0:T(8,128)(2,1)} %maximum_select_fusion.2, bf16[512,1536]{1,0:T(8,128)(2,1)} %collective-permute-done.1, pred[]{:T(512)S(6)} %ne.4), kind=kOutput, calls=%fused_computation.2 | convolution fusion | flops 2839609344 | bytes 7733249 | tf_op jit(solution)/shard_map/dot_general | solution.py:20
  392.9 5.3 convolution_convert_fusion
  401.1 6.3 convolution_convert_fusion.2
  407.5 2.1 fusion.1
  409.8 1.5 collective-permute-start.6
  411.3 16.8 %collective-permute-done.6 = bf16[1,256,1536]{2,1,0:T(8,128)(2,1)S(1)} collective-permute-done((bf16[1,256,1536]{2,1,0:T(8,128)(2,1)S(1)}, bf16[1,256,1536]{2,1,0:T(8,128)(2,1)S(1)}, u32[]{:S(2)}, u32[]{:S(2)}) %collective-permute-start.6) | collective-permute-done | bytes 786464 | tf_op jit(solution)/shard_map/ppermute | solution.py:360
  428.2 2.2 fusion.19
  431.4 49.8 %reduce-scatter.6.cloned.1.call-done = bf16[192,768]{1,0:T(8,128)(2,1)} async-done(((bf16[1536,768]{1,0:T(8,128)(2,1)}), bf16[192,768]{1,0:T(8,128)(2,1)}) %reduce-scatter.6.cloned.1.call-update) | async-done | bytes 294928 | tf_op jit(solution)/shard_map/reduce_scatter | solution.py:509
  481.2 74.7 %reduce-scatter.4.cloned.1.call-done = bf16[192,896]{1,0:T(8,128)(2,1)} async-done(((bf16[1536,896]{1,0:T(8,128)(2,1)}), bf16[192,896]{1,0:T(8,128)(2,1)}) %reduce-scatter.4.cloned.1.call-update) | async-done | bytes 344080 | tf_op jit(solution)/shard_map/reduce_scatter | solution.py:527
  555.9 1.9 pad_maximum_fusion.2
  557.9 3.5 all-to-all-start.1
  565.4 62.5 %reduce-scatter.8.cloned.1.call-done = bf16[96,1536]{1,0:T(8,128)(2,1)} async-done(((bf16[768,1536]{1,0:T(8,128)(2,1)}), bf16[96,1536]{1,0:T(8,128)(2,1)}) %reduce-scatter.8.cloned.1.call-update) | async-done | bytes 294928 | tf_op jit(solution)/shard_map/reduce_scatter | solution.py:508
  627.8 1.9 collective-permute-start.11
  630.4 17.2 %collective-permute-done.11 = bf16[96,1536]{1,0:T(8,128)(2,1)S(1)} collective-permute-done((bf16[96,1536]{1,0:T(8,128)(2,1)}, bf16[96,1536]{1,0:T(8,128)(2,1)S(1)}, u32[]{:S(2)}, u32[]{:S(2)}) %collective-permute-start.11) | collective-permute-done | bytes 294944 | tf_op jit(solution)/shard_map/ppermute | solution.py:510
  (191 shorter events, 35.5 us)
Async XLA Ops:
  7.2 83.2 %all-gather.9.cloned.1.call-start = ((), (), s32[]{:S(2)}) async-start(), calls=%async_computation.6 | async-start | bytes 2654208 | tf_op jit(solution)/shard_map/all_gather | solution.py:433
  9.1 15.4 %copy-start = (bf16[1,256,1536]{2,1,0:T(8,128)(2,1)S(1)}, bf16[1,256,1536]{2,1,0:T(8,128)(2,1)}, u32[]{:S(2)}) copy-start(bf16[1,256,1536]{2,1,0:T(8,128)(2,1)} %param.12) | copy-start | bytes 2359300
  9.3 15.5 %copy-start.19 = (f32[1536]{0:T(1024)S(1)}, f32[1536]{0:T(1024)}, u32[]{:S(2)}) copy-start(f32[1536]{0:T(1024)} %param.15) | copy-start | bytes 18436
  23.6 6.0 copy-start.13
  23.6 124.2 %all-gather.7.cloned.1.call-start = ((), (), s32[]{:S(2)}) async-start(), calls=%async_computation.5 | async-start | bytes 3096576 | tf_op jit(solution)/shard_map/all_gather | solution.py:432
  24.4 176.6 %all-gather.11.cloned.1.call-start = ((), (), s32[]{:S(2)}) async-start(), calls=%async_computation.7 | async-start | bytes 2654208 | tf_op jit(solution)/shard_map/all_gather | solution.py:437
  24.7 23.7 %copy-start.5 = (bf16[1,256,1536]{2,1,0:T(8,128)(2,1)S(1)}, bf16[1,256,1536]{2,1,0:T(8,128)(2,1)}, u32[]{:S(2)}) copy-start(bf16[1,256,1536]{2,1,0:T(8,128)(2,1)} %param.14) | copy-start | bytes 2359300
  24.7 39.0 %copy-start.21 = (s32[1,256]{1,0:T(1,128)S(1)}, s32[1,256]{1,0:T(1,128)}, u32[]{:S(2)}) copy-start(s32[1,256]{1,0:T(1,128)} %param.13) | copy-start | bytes 3076
  24.7 45.5 %copy-start.22 = (f32[48]{0:T(128)S(1)}, f32[48]{0:T(128)}, u32[]{:S(2)}) copy-start(f32[48]{0:T(128)} %param.20) | copy-start | bytes 580
  24.7 45.5 %copy-start.23 = (f32[48]{0:T(128)S(1)}, f32[48]{0:T(128)}, u32[]{:S(2)}) copy-start(f32[48]{0:T(128)} %param.19) | copy-start | bytes 580
  24.7 45.5 %slice-start.3 = ((f32[3328]{0:T(1024)}), f32[3072]{0:T(1024)S(1)}, s32[]{:S(2)}) async-start(f32[3328]{0:T(1024)} %param.18), calls=%async_computation.16 | async-start | bytes 24576 | tf_op jit(solution)/shard_map/slice | solution.py:457
  24.7 47.2 %copy-start.26 = (f32[48]{0:T(128)S(1)}, f32[48]{0:T(128)}, u32[]{:S(2)}) copy-start(f32[48]{0:T(128)} %param.21) | copy-start | bytes 580
  24.8 48.8 %slice-start.2 = ((f32[3328]{0:T(1024)}), f32[256]{0:T(256)S(1)}, s32[]{:S(2)}) async-start(f32[3328]{0:T(1024)} %param.18), calls=%async_computation.15 | async-start | bytes 2048 | tf_op jit(solution)/shard_map/slice | solution.py:459
  24.8 48.9 %slice-start = ((f32[4,3328]{1,0:T(4,128)}), f32[4,256]{1,0:T(4,128)S(1)}, s32[]{:S(2)}) async-start(f32[4,3328]{1,0:T(4,128)} %param.17), calls=%async_computation.13 | async-start | bytes 8192 | tf_op jit(solution)/shard_map/slice | solution.py:458
  24.8 48.9 %slice-start.1 = ((f32[4,3328]{1,0:T(4,128)}), f32[4,3072]{1,0:T(4,128)S(1)}, s32[]{:S(2)}) async-start(f32[4,3328]{1,0:T(4,128)} %param.17), calls=%async_computation.14 | async-start | bytes 98304 | tf_op jit(solution)/shard_map/slice | solution.py:456
  25.1 2.4 collective-permute-start
  29.2 49.2 %collective-permute-start.1 = (bf16[512,1536]{1,0:T(8,128)(2,1)}, bf16[512,1536]{1,0:T(8,128)(2,1)}, u32[]{:S(2)}, u32[]{:S(2)}) collective-permute-start(bf16[512,1536]{1,0:T(8,128)(2,1)} %maximum_select_fusion.2), channel_id=1, source_target_pairs={{0,2},{1,3},{2,0},{3,1},{4,6},{5,7},{6,4},{7,5},{8,10},{9,11},{10,... | collective-permute-start | bytes 4718600 | tf_op jit(solution)/shard_map/ppermute | solution.py:360
  29.6 18.0 %collective-permute-start.4 = (bf16[96,1536]{1,0:T(8,128)(2,1)S(1)}, bf16[96,1536]{1,0:T(8,128)(2,1)S(1)}, u32[]{:S(2)}, u32[]{:S(2)}) collective-permute-start(bf16[96,1536]{1,0:T(8,128)(2,1)S(1)} %convert_element_type.177), channel_id=1, source_target_pairs={{0,0},{1,4},{2,8},{3,12},{4,16},{5,20},{6,24},{7,28},{8,1},{9,5},{... | collective-permute-start | bytes 884744 | tf_op jit(solution)/shard_map/ppermute | solution.py:436
  48.4 326.1 %all-reduce.16.cloned.1.call-start = ((), (), s32[]{:S(2)}) async-start(), calls=%async_computation.11 | async-start | bytes 417792
  48.4 26.0 %collective-permute-start.2 = (bf16[256,1536]{1,0:T(8,128)(2,1)S(1)}, bf16[256,1536]{1,0:T(8,128)(2,1)S(1)}, u32[]{:S(2)}, u32[]{:S(2)}) collective-permute-start(bf16[256,1536]{1,0:T(8,128)(2,1)S(1)} %bitcast.173), channel_id=1, source_target_pairs={{0,1},{1,0},{2,3},{3,2},{4,5},{5,4},{6,7},{7,6},{8,9},{9,8},{10,11... | collective-permute-start | bytes 2359304 | tf_op jit(solution)/shard_map/ppermute | solution.py:360
  75.0 23.4 %copy-start.8 = (bf16[512,1536]{1,0:T(8,128)(2,1)}, bf16[512,1536]{1,0:T(8,128)(2,1)S(1)}, u32[]{:S(2)}) copy-start(bf16[512,1536]{1,0:T(8,128)(2,1)S(1)} %maximum_select_fusion.3) | copy-start | bytes 4718596
  75.0 109.5 %collective-permute-start.3 = (bf16[512,1536]{1,0:T(8,128)(2,1)S(1)}, bf16[512,1536]{1,0:T(8,128)(2,1)}, u32[]{:S(2)}, u32[]{:S(2)}) collective-permute-start(bf16[512,1536]{1,0:T(8,128)(2,1)S(1)} %maximum_select_fusion.3), channel_id=1, source_target_pairs={{0,2},{1,3},{2,0},{3,1},{4,6},{5,7},{6,4},{7,5},{8,10},{9,11},{10,... | collective-permute-start | bytes 4718600 | tf_op jit(solution)/shard_map/ppermute | solution.py:360
  152.0 17.5 %copy-start.10 = (f32[1024,128]{0,1:T(8,128)}, f32[1024,128]{0,1:T(8,128)S(1)}, u32[]{:S(2)}) copy-start(f32[1024,128]{0,1:T(8,128)S(1)} %fusion.27) | copy-start | bytes 1572868
  211.1 12.3 %copy-start.3 = (f32[1024,768]{1,0:T(8,128)}, f32[1024,768]{1,0:T(8,128)S(1)}, u32[]{:S(2)}) copy-start(f32[1024,768]{1,0:T(8,128)S(1)} %get-tuple-element.39) | copy-start | bytes 9437188
  254.1 6.1 copy-start.18
  254.1 9.9 %copy-start.11 = (f32[1024,64]{0,1:T(8,128)S(1)}, f32[1024,64]{0,1:T(8,128)}, u32[]{:S(2)}) copy-start(f32[1024,64]{0,1:T(8,128)} %get-tuple-element.41) | copy-start | bytes 786436
  255.4 1.6 collective-permute-start.7
  258.4 5.6 collective-permute-start.8
  260.2 11.7 %copy-start.16 = (bf16[1024,64]{1,0:T(8,128)(2,1)}, bf16[1024,64]{1,0:T(8,128)(2,1)S(1)}, u32[]{:S(2)}) copy-start(bf16[1024,64]{1,0:T(8,128)(2,1)S(1)} %slice.433) | copy-start | bytes 393220
  266.0 5.9 copy-start.7
  275.0 6.8 %copy-start.28 = (u32[32]{0:T(128)S(1)}, u32[32]{0:T(128)}, u32[]{:S(2)}) copy-start(u32[32]{0:T(128)} %constant.74) | copy-start | bytes 388
  275.1 8.0 %copy-start.20 = (f32[8,768]{1,0:T(8,128)S(1)}, f32[8,768]{1,0:T(8,128)}, u32[]{:S(2)}) copy-start(f32[8,768]{1,0:T(8,128)} %get-tuple-element.23) | copy-start | bytes 73732
  275.1 3.5 collective-permute-start.9
  280.1 19.9 %collective-permute-start.10 = (bf16[1,256,1536]{2,1,0:T(8,128)(2,1)}, bf16[1,256,1536]{2,1,0:T(8,128)(2,1)}, u32[]{:S(2)}, u32[]{:S(2)}) collective-permute-start(bf16[1,256,1536]{2,1,0:T(8,128)(2,1)} %fusion.22), channel_id=1, source_target_pairs={{0,2},{1,3},{2,0},{3,1},{4,6},{5,7},{6,4},{7,5},{8,10},{9,11},{10,... | collective-permute-start | bytes 2359304 | tf_op jit(solution)/shard_map/ppermute | solution.py:360
  284.2 20.5 %copy-start.27 = (u32[32]{0:T(128)S(1)}, u32[32]{0:T(128)}, u32[]{:S(2)}) copy-start(u32[32]{0:T(128)} %constant.79) | copy-start | bytes 388
  304.4 125.9 %all-reduce.18.cloned.1.call-start = ((), (), s32[]{:S(2)}) async-start(), calls=%async_computation.12 | async-start | bytes 212992
  376.9 7.7 %copy-start.17 = (bf16[1024,64]{1,0:T(8,128)(2,1)S(1)}, bf16[1024,64]{1,0:T(8,128)(2,1)}, u32[]{:S(2)}) copy-start(bf16[1024,64]{1,0:T(8,128)(2,1)} %copy-done.16) | copy-start | bytes 393220
  376.9 7.7 %copy-start.25 = (bf16[1024,768]{1,0:T(8,128)(2,1)S(1)}, bf16[1024,768]{1,0:T(8,128)(2,1)}, u32[]{:S(2)}) copy-start(bf16[1024,768]{1,0:T(8,128)(2,1)} %get-tuple-element.20) | copy-start | bytes 4718596
  376.9 104.3 %reduce-scatter.6.cloned.1.call-start = ((), (), s32[]{:S(2)}) async-start(), calls=%async_computation.9 | async-start | bytes 2654208 | tf_op jit(solution)/shard_map/reduce_scatter | solution.py:509
  384.5 171.4 %reduce-scatter.4.cloned.1.call-start = ((), (), s32[]{:S(2)}) async-start(), calls=%async_computation.8 | async-start | bytes 3096576 | tf_op jit(solution)/shard_map/reduce_scatter | solution.py:527
  392.6 235.2 %reduce-scatter.8.cloned.1.call-start = ((), (), s32[]{:S(2)}) async-start(), calls=%async_computation.10 | async-start | bytes 2654208 | tf_op jit(solution)/shard_map/reduce_scatter | solution.py:508
  399.5 8.0 %collective-permute-start.5 = (bf16[2,256,1536]{2,1,0:T(8,128)(2,1)}, bf16[2,256,1536]{2,1,0:T(8,128)(2,1)}, u32[]{:S(2)}, u32[]{:S(2)}) collective-permute-start(bf16[2,256,1536]{2,1,0:T(8,128)(2,1)} %select_bitcast_fusion.1), channel_id=1, source_target_pairs={{0,1},{1,0},{2,3},{3,2},{4,5},{5,4},{6,7},{7,6},{8,9},{9,8},{10,11... | collective-permute-start | bytes 4718600 | tf_op jit(solution)/shard_map/ppermute | solution.py:360
  407.5 20.7 %copy-start.1 = (bf16[1,256,1536]{2,1,0:T(8,128)(2,1)S(1)}, bf16[1,256,1536]{2,1,0:T(8,128)(2,1)}, u32[]{:S(2)}) copy-start(bf16[1,256,1536]{2,1,0:T(8,128)(2,1)} %param.12) | copy-start | bytes 2359300
  407.5 20.7 %copy-start.6 = (bf16[1,256,1536]{2,1,0:T(8,128)(2,1)S(1)}, bf16[1,256,1536]{2,1,0:T(8,128)(2,1)}, u32[]{:S(2)}) copy-start(bf16[1,256,1536]{2,1,0:T(8,128)(2,1)} %param.14) | copy-start | bytes 2359300
  409.6 18.6 %copy-start.2 = (f32[1,256,1536]{2,1,0:T(8,128)S(1)}, f32[1,256,1536]{2,1,0:T(8,128)}, u32[]{:S(2)}) copy-start(f32[1,256,1536]{2,1,0:T(8,128)} %get-tuple-element.38) | copy-start | bytes 4718596
  409.8 18.4 %collective-permute-start.6 = (bf16[1,256,1536]{2,1,0:T(8,128)(2,1)S(1)}, bf16[1,256,1536]{2,1,0:T(8,128)(2,1)S(1)}, u32[]{:S(2)}, u32[]{:S(2)}) collective-permute-start(bf16[1,256,1536]{2,1,0:T(8,128)(2,1)S(1)} %fusion.21), channel_id=1, source_target_pairs={{0,2},{1,3},{2,0},{3,1},{4,6},{5,7},{6,4},{7,5},{8,10},{9,11},{10,... | collective-permute-start | bytes 2359304 | tf_op jit(solution)/shard_map/ppermute | solution.py:360
  557.9 90.6 %all-to-all-start.1 = ((bf16[4,48,1664]{2,1,0:T(8,128)(2,1)}), bf16[4,48,1664]{2,1,0:T(8,128)(2,1)S(1)}, u32[]{:S(2)}, u32[]{:S(2)}) async-start(bf16[4,48,1664]{2,1,0:T(8,128)(2,1)} %bitcast.46), calls=%async_computation.3 | async-start | bytes 1277952 | tf_op jit(solution)/shard_map/all_to_all | solution.py:532
  627.8 19.7 %collective-permute-start.11 = (bf16[96,1536]{1,0:T(8,128)(2,1)}, bf16[96,1536]{1,0:T(8,128)(2,1)S(1)}, u32[]{:S(2)}, u32[]{:S(2)}) collective-permute-start(bf16[96,1536]{1,0:T(8,128)(2,1)} %reduce-scatter.8.cloned.1.call-done), channel_id=1, source_target_pairs={{0,0},{4,1},{8,2},{12,3},{16,4},{20,5},{24,6},{28,7},{1,8},{5,9},{... | collective-permute-start | bytes 884744 | tf_op jit(solution)/shard_map/ppermute | solution.py:510
  (6 other events, 13.4 us)
Sparse Core Ops, SparseCore 0:
  23.7 66.7 all-gather.8
  93.2 54.5 all-gather.6
  150.5 50.4 all-gather.10
  304.6 69.9 all-reduce.15
  377.3 30.1 all-reduce.17
  410.8 70.4 reduce-scatter.5
  484.8 71.0 reduce-scatter.3
  559.4 68.3 reduce-scatter.7

commit v2 on v1

--- a/solution.py
+++ b/solution.py
@@ -394,6 +394,25 @@
     return held[0]
 
 
+def summed(block):
+    count = lax.axis_size("dp")
+    for bit in bits_of(count):
+        block = block + lax.ppermute(block, "dp", [(i, i ^ bit) for i in range(count)])
+    return block
+
+
+def folded(rows, lead, width):
+    cut = rows.reshape(lead, rows.shape[0] // lead, rows.shape[1] // width, width)
+    cut = cut.transpose(0, 2, 1, 3).reshape(lead, -1, width)
+    return cut[0] if lead == 1 else cut
+
+
+def unfolded(pieces, width):
+    lead, stacked, narrow = pieces.shape
+    cut = pieces.reshape(lead, width // narrow, stacked * narrow // width, narrow)
+    return cut.transpose(0, 2, 1, 3).reshape(-1, width)
+
+
 def padded(rows, width):
     return jnp.pad(rows, ((0, 0), (0, width - rows.shape[1])))
 
@@ -430,16 +449,20 @@
     mine = mine.reshape(size * in_rows, -1)
     n_first = own_inner + LANES
     w_first = lax.all_gather(mine[:, :n_first], "dp", axis=0, tiled=True)
-    w_z = lax.all_gather(mine[:, n_first:], "dp", axis=0, tiled=True)
     order = [(f, (f % groups) * size + f // groups) for f in range(groups * size)]
     back = [(b, a) for a, b in order]
     out_moved = lax.ppermute(out_weight.astype(bf16), ("dp", "seq"), order)
-    w_out = lax.all_gather(out_moved, "dp", axis=0, tiled=True)
+    z_block = jnp.concatenate([mine[:, n_first:], folded(out_moved, 1, own_inner)], axis=0)
 
     flat = hidden.reshape(block, n_width).astype(f32)
     inv = lax.rsqrt(jnp.mean(flat * flat, axis=-1, keepdims=True) + epsilon)
     unit = flat * inv
     normed = gathered((unit * norm_gain).astype(bf16))
+    normed, z_block = lax.optimization_barrier((normed, z_block))
+    joined = lax.all_gather(z_block, "dp", axis=0, tiled=True).reshape(groups, -1, own_inner)
+    z_rows = size * in_rows
+    w_z = joined[:, :z_rows].reshape(-1, own_inner)
+    w_out = unfolded(joined[:, z_rows:], n_width)
     cot_own = cotangent.reshape(block, n_width)
     cot = gathered(cot_own)
     docs = lax.all_gather(segments.reshape(block), "seq", axis=0, tiled=True).astype(f32)
@@ -504,9 +527,12 @@
     branch = scattered(mm(gate_low, w_out, NN).astype(bf16))
     result = (flat + branch).reshape(n_seqs, block, n_width).astype(bf16)
     out_term = mm(gate_low, cot, TN).astype(bf16)
-    z_term = mm(normed, d_z, TN).astype(bf16)
-    out_part = lax.psum_scatter(out_term, "dp", scatter_dimension=0, tiled=True)
-    z_part = lax.psum_scatter(z_term, "dp", scatter_dimension=0, tiled=True)
+    z_term = mm(normed, d_z, TN).astype(bf16).reshape(groups, z_rows, own_inner)
+    terms = jnp.concatenate([z_term, folded(out_term, groups, own_inner)], axis=1)
+    terms, d_y = lax.optimization_barrier((terms.reshape(-1, own_inner), d_y))
+    parts = lax.psum_scatter(terms, "dp", scatter_dimension=0, tiled=True)
+    z_part = parts[:z_rows]
+    out_part = unfolded(parts[None, z_rows:], n_width)
     d_out_weight = lax.ppermute(out_part, ("dp", "seq"), back).astype(f32)
 
     d_x, d_dt, d_bct, d_conv_x, d_heads = run_backward(
@@ -559,8 +585,7 @@
             d_norm_gain,
         ]
     )
-    packed = jnp.sum(lax.all_gather(packed, "dp", axis=0), axis=0)
-    packed = lax.all_gather(packed, "seq", axis=0)
+    packed = gathered(summed(packed)[None])
     at = 0
 
     def take(count):

time: 664 us -> 445 us (0.67)
  waiting for transfers between devices: 408 us -> 168 us
  other arithmetic: 33.8 us -> 53.3 us
  matrix products: 65.6 us -> 48.9 us
  blocking collectives: 33.1 us -> 49.3 us
  local copies, waits for them, and re-layouts: 21.6 us -> 36.2 us
  starting transfers between devices: 35 us -> 24.9 us
    reduce_scatter x2 -> x1, waiting for transfers between devices: 112 us -> 0.01 us  [shards(): parts = lax.psum_scatter(terms, 'dp', scatter_dimension=0, tiled=True)]
    unnamed x10 -> x4, waiting for transfers between devices: 68.7 us -> 0.07 us
    all_gather x1, waiting for transfers between devices: 49.3 us -> 7.72 us  [shards(): w_first = lax.all_gather(mine[:, :n_first], 'dp', axis=0, tiled=True)]
    reduce_scatter x1, waiting for transfers between devices: 74.7 us -> 42.4 us  [shards(): lax.psum_scatter(first_term, 'dp', scatter_dimension=0, tiled=True)]
    dot_general x10, matrix products: 65.6 us -> 48.9 us  [mm(): return lax.dot_general(a, b, (dims, ((), ())), preferred_element_type=out)]
    all_gather x1, blocking collectives: 8.11 us -> 24.7 us  [shards(): lax.all_gather((bc_conv * bc_sig).astype(bf16).T, 'seq', axis=0, tiled=True)]
    ppermute x10 -> x12, starting transfers between devices: 24.4 us -> 8.41 us  [swapped(): return lax.ppermute(block, 'seq', [(i, i ^ bit) for i in range(size)])]
    ppermute x10 -> x12, waiting for transfers between devices: 43.6 us -> 58.1 us  [swapped(): return lax.ppermute(block, 'seq', [(i, i ^ bit) for i in range(size)])]
  transfers between devices with their start and end apart: 21 -> 22, of which waited for: 15 -> 14; matrix products, arithmetic and copies ran while one was open for 11% -> 20% of each run, Pallas kernels for 2% -> 10%
where the time goes in v2:
time: 445 us; the launch traced here: 440 us
  waiting for transfers between devices  168 us (38%)
  other arithmetic  53.3 us (12%)
  blocking collectives  49.3 us (11%)
  matrix products  48.9 us (11%)
  Pallas kernels  44.1 us (10%)
  local copies, waits for them, and re-layouts  36.2 us (8%)
  starting transfers between devices  24.9 us (6%)
  between operations  14.9 us (3%)
    ppermute x12, waiting for transfers between devices, swapped(): return lax.ppermute(block, 'seq', [(i, i ^ bit) for i in range(size)])  58.1 us
    dot_general x10, matrix products, mm(): return lax.dot_general(a, b, (dims, ((), ())), preferred_element_type=out)  48.9 us
    reduce_scatter x1, waiting for transfers between devices, shards(): lax.psum_scatter(first_term, 'dp', scatter_dimension=0, tiled=True)  42.4 us
    pallas_call x1, Pallas kernels, run_backward(): pl.pallas_call(functools.partial(scan_backward, q, taps, pairs, head, chu...  30.7 us
    all_gather x1, waiting for transfers between devices, shards(): lax.all_gather(z_block, 'dp', axis=0, tiled=True)  26.8 us
    all_gather x1, blocking collectives, shards(): lax.all_gather((bc_conv * bc_sig).astype(bf16).T, 'seq', axis=0, tiled=True)  24.7 us
    ppermute x1, waiting for transfers between devices, shards(): d_out_weight = lax.ppermute(out_part, ('dp', 'seq'), back).astype(f32)  15.6 us
    ppermute x1, waiting for transfers between devices, shards(): out_moved = lax.ppermute(out_weight.astype(bf16), ('dp', 'seq'), order)  13.5 us
  transfers between devices with their start and end apart: 22, of which 14 were waited for; matrix products, arithmetic and copies ran while one was open for 20% of the time, Pallas kernels for 10%

profile of v2, /device:TPU:2, one launch (start us, length us, event | category | flops | bytes accessed | tf_op | source)
XLA Modules:
  0.0 439.7 jit_solution(1094193148376527668)
XLA Ops:
  10.2 12.6 %all_to_all.10 = bf16[4,48,1664]{2,1,0:T(8,128)(2,1)S(1)} all-to-all(bf16[4,48,1664]{2,1,0:T(8,128)(2,1)S(1)} %copy.107), channel_id=1, replica_groups=mesh['dp'=8,'seq'=4] {'seq'}, dimensions={0} | all-to-all | bytes 1277952 | tf_op jit(solution)/shard_map/all_to_all | solution.py:448
  24.2 2.4 collective-permute-done
  26.6 1.9 maximum_select_fusion.2
  30.2 4.5 %collective-permute-start.2 = (bf16[96,1536]{1,0:T(8,128)(2,1)S(1)}, bf16[96,1536]{1,0:T(8,128)(2,1)S(1)}, u32[]{:S(2)}, u32[]{:S(2)}) collective-permute-start(bf16[96,1536]{1,0:T(8,128)(2,1)S(1)} %convert_element_type.173), channel_id=1, source_target_pairs={{0,0},{1,4},{2,8},{3,12},{4,16},{5,20},{6,24},{7,28},{8,1},{9,5},{... | collective-permute-start | bytes 884744 | tf_op jit(solution)/shard_map/ppermute | solution.py:454
  34.6 13.5 %collective-permute-done.2 = bf16[96,1536]{1,0:T(8,128)(2,1)S(1)} collective-permute-done((bf16[96,1536]{1,0:T(8,128)(2,1)S(1)}, bf16[96,1536]{1,0:T(8,128)(2,1)S(1)}, u32[]{:S(2)}, u32[]{:S(2)}) %collective-permute-start.2) | collective-permute-done | bytes 294944 | tf_op jit(solution)/shard_map/ppermute | solution.py:454
  49.3 20.0 %collective-permute-done.1 = bf16[512,1536]{1,0:T(8,128)(2,1)} collective-permute-done((bf16[512,1536]{1,0:T(8,128)(2,1)S(1)}, bf16[512,1536]{1,0:T(8,128)(2,1)}, u32[]{:S(2)}, u32[]{:S(2)}) %collective-permute-start.1) | collective-permute-done | bytes 1572896 | tf_op jit(solution)/shard_map/ppermute | solution.py:360
  69.3 3.3 maximum_select_fusion
  72.7 6.0 %all-gather = s32[1,1024]{1,0:T(1,128)S(1)} all-gather(s32[1,256]{1,0:T(1,128)S(1)} %copy-done.33), channel_id=2, replica_groups=mesh['dp'=8,'seq'=4] {'seq'}, dimensions={1}, use_global_device_ids=true | all-gather | bytes 5120 | tf_op jit(solution)/shard_map/all_gather | solution.py:468
  82.9 3.5 maximum_select_fusion.3
  88.0 7.7 %all-gather.4.cloned.1.call-done = bf16[1536,896]{1,0:T(8,128)(2,1)} async-done(((bf16[192,896]{1,0:T(8,128)(2,1)}), bf16[1536,896]{1,0:T(8,128)(2,1)}) %all-gather.4.cloned.1.call-update) | async-done | bytes 2752528 | tf_op jit(solution)/shard_map/all_gather | solution.py:451
  95.7 3.0 fusion.27
  98.7 2.0 copy.109
  102.7 24.7 %all_gather.14.bct_ref = bf16[256,1024]{1,0:T(8,128)(2,1)} all-gather(bf16[64,1024]{1,0:T(8,128)(2,1)S(1)} %get-tuple-element.48), channel_id=1, replica_groups=mesh['dp'=8,'seq'=4] {'seq'}, dimensions={0}, use_global_device_ids=true | all-gather | bytes 655360 | tf_op jit(solution)/shard_map/all_gather | solution.py:506
  127.4 1.9 broadcast_select_fusion.small_ref
  129.3 5.3 %fusion.10.x_ref.xp_ref = bf16[1024,768]{1,0:T(8,128)(2,1)} fusion(bf16[1024,1536]{1,0:T(8,128)(2,1)S(1)} %maximum_select_fusion, bf16[1536,896]{1,0:T(8,128)(2,1)} %all-gather.4.cloned.1.call-done), kind=kOutput, calls=%fused_computation.31 | convolution fusion | flops 2416705536 | bytes 7077888 | tf_op jit(solution)/shard_map/dot_general | solution.py:20
  136.2 13.4 %scan_forward.1 = (f32[1024,768]{1,0:T(8,128)}, f32[8,128,768]{2,1,0:T(8,128)}) custom-call(bf16[1024,768]{1,0:T(8,128)(2,1)} %fusion.10.x_ref.xp_ref, f32[1024,128]{1,0:T(8,128)} %broadcast_select_fusion.small_ref, bf16[256,1024]{1,0:T(8,128)(2,1)} %all_gather.14.bct_ref, f32[1024,128]{1,0:T(8,128)} %broadcast_in_dim.62.dcol_ref.dcolp_ref, ...), custom_call_target="tpu_custom_call" | custom-call | tf_op jit(solution)/shard_map/scan_forward/pallas_call | solution.py:270
  149.7 26.8 %all-gather.6.cloned.1.call-done = bf16[3072,768]{1,0:T(8,128)(2,1)} async-done(((bf16[384,768]{1,0:T(8,128)(2,1)}), bf16[3072,768]{1,0:T(8,128)(2,1)}) %all-gather.6.cloned.1.call-update) | async-done | bytes 4718608 | tf_op jit(solution)/shard_map/all_gather | solution.py:462
  176.4 2.7 fusion.58
  179.1 2.4 copy.112
  182.0 2.6 fusion.62
  184.8 9.4 %multiply_reduce_fusion.2 = (f32[1024]{0:T(1024)S(1)}, f32[1024]{0:T(1024)S(1)}, f32[1024,768]{1,0:T(8,128)}, f32[1024,768]{1,0:T(8,128)}) fusion(f32[768]{0:T(1024)S(1)} %dynamic-slice.23, f32[1024,768]{1,0:T(8,128)S(1)} %copy-done.8, f32[1024,768]{1,0:T(8,128)S(1)} %fusion.62, bf16[768,1536]{1,0:T(8,128)(2,1)S(1)} %bitcast.209, ...), kind=kOutput, calls=%fused_computation.17 | convolution fusion | flops 2437937152 | bytes 18099200 | tf_op jit(solution)/shard_map/dot_general | solution.py:20
  194.2 5.9 %psum.7 = f32[2,1024]{1,0:T(2,128)S(1)} all-reduce(f32[2,1024]{1,0:T(2,128)S(1)} %pad_maximum_fusion.8), channel_id=1, replica_groups=mesh['dp'=8,'seq'=4] {'seq'}, use_global_device_ids=true, to_apply=%region_3.4 | all-reduce | flops 2048 | bytes 16384 | tf_op jit(solution)/shard_map/psum | solution.py:518
  200.2 7.5 %fusion.20 = (f32[1024,768]{1,0:T(8,128)}, bf16[1024,768]{1,0:T(8,128)(2,1)S(1)}, f32[768]{0:T(1024)}) fusion(f32[1024,768]{1,0:T(8,128)} %get-tuple-element.47, f32[1024]{0:T(1024)S(1)} %fusion.42, f32[1024,768]{1,0:T(8,128)} %get-tuple-element.78, f32[1024]{0:T(1024)S(1)} %bitcast.228, f32[768]{0:T(1024)S(1)} %dynamic-slice.23, f32[1024,768]{1,0:T(8,128)} %copy-done.9, ...), kind=kLoop, calls=%fused_computation.52 | loop fusion | flops 14941440 | bytes 17315840 | tf_op jit(solution)/shard_map/mul | solution.py:525
  208.9 3.9 convolution_convert_fusion.3
  212.8 7.4 %convolution_convert_fusion.2 = bf16[768,1536]{1,0:T(8,128)(2,1)} fusion(bf16[512,1536]{1,0:T(8,128)(2,1)} %maximum_select_fusion.3, bf16[512,1536]{1,0:T(8,128)(2,1)} %collective-permute-done.4, pred[]{:T(512)S(6)} %ne.4, f32[1024,768]{1,0:T(8,128)S(1)} %copy-done.6, f32[1024]{0:T(1024)S(1)} %bitcast.229, f32[768]{0:T(1024)S(1)} %dynamic-slice.23), kind=kOutput, calls=%fused_computation.4 | convolution fusion | flops 2433613824 | bytes 8657921 | tf_op jit(solution)/shard_map/dot_general | solution.py:20
  220.3 6.0 %reshape.399 = bf16[8,96,2,768]{3,2,1,0:T(2,128)(2,1)} reshape(bf16[768,1536]{1,0:T(8,128)(2,1)} %convolution_convert_fusion.2) | data formatting | bytes 4718592 | tf_op jit(solution)/shard_map/reshape | solution.py:405
  226.3 2.2 copy.116
  228.6 2.5 pad_maximum_fusion
  231.4 30.7 %scan_backward.1 = (bf16[1024,768]{1,0:T(8,128)(2,1)}, f32[1024,128]{1,0:T(8,128)}, f32[256,1024]{1,0:T(8,128)}, f32[8,768]{1,0:T(8,128)}, f32[8,128]{1,0:T(8,128)}) custom-call(bf16[1024,768]{1,0:T(8,128)(2,1)} %fusion.10.x_ref.xp_ref, bf16[1024,768]{1,0:T(8,128)(2,1)} %fusion.10.x_ref.xp_ref, f32[1024,128]{1,0:T(8,128)} %broadcast_select_fusion.small_ref, ...), custom_call_target="tpu_custom_call" | custom-call | tf_op jit(solution)/shard_map/scan_backward/pallas_call | solution.py:315
  268.9 3.1 collective-permute-done.8
  272.9 1.9 fusion.56
  275.0 6.0 %fusion.23 = f32[1024,1536]{1,0:T(8,128)S(1)} fusion(bf16[1536,896]{1,0:T(8,128)(2,1)} %all-gather.4.cloned.1.call-done, bf16[1024,64]{1,0:T(8,128)(2,1)S(1)} %copy.119, bf16[1024,64]{1,0:T(8,128)(2,1)} %slice.453, bf16[1024,768]{1,0:T(8,128)(2,1)} %get-tuple-element.27), kind=kOutput, calls=%fused_computation.58 | convolution fusion | flops 2824077312 | bytes 10878976 | tf_op jit(solution)/shard_map/dot_general | solution.py:20
  281.1 3.0 add_convert_fusion
  285.4 2.3 copy-done.7
  287.7 3.0 convolution_convert_fusion
  293.8 5.2 %convolution_convert_fusion.1 = bf16[1536,896]{1,0:T(8,128)(2,1)} fusion(bf16[1024,1536]{1,0:T(8,128)(2,1)S(1)} %maximum_select_fusion, bf16[1024,64]{1,0:T(8,128)(2,1)S(1)} %copy.119, bf16[1024,64]{1,0:T(8,128)(2,1)S(1)} %copy-done.19, bf16[1024,768]{1,0:T(8,128)(2,1)S(1)} %copy-done.36), kind=kOutput, calls=%fused_computation.3 | convolution fusion | flops 2825453568 | bytes 7733248 | tf_op jit(solution)/shard_map/dot_general | solution.py:20
  299.1 3.0 fusion
  306.0 17.4 %collective-permute-done.10 = bf16[1,256,1536]{2,1,0:T(8,128)(2,1)} collective-permute-done((bf16[1,256,1536]{2,1,0:T(8,128)(2,1)}, bf16[1,256,1536]{2,1,0:T(8,128)(2,1)}, u32[]{:S(2)}, u32[]{:S(2)}) %collective-permute-start.10) | collective-permute-done | bytes 786464 | tf_op jit(solution)/shard_map/ppermute | solution.py:360
  323.4 3.0 fusion.14
  328.0 2.4 collective-permute-done.11
  331.4 3.1 fusion.1
  334.5 2.6 collective-permute-start.13
  342.6 12.6 %collective-permute-done.6 = bf16[1,256,1536]{2,1,0:T(8,128)(2,1)S(1)} collective-permute-done((bf16[1,256,1536]{2,1,0:T(8,128)(2,1)S(1)}, bf16[1,256,1536]{2,1,0:T(8,128)(2,1)S(1)}, u32[]{:S(2)}, u32[]{:S(2)}) %collective-permute-start.6) | collective-permute-done | bytes 786464 | tf_op jit(solution)/shard_map/ppermute | solution.py:360
  355.3 2.2 fusion.19
  358.7 42.4 %reduce-scatter.3.cloned.1.call-done = bf16[192,896]{1,0:T(8,128)(2,1)} async-done(((bf16[1536,896]{1,0:T(8,128)(2,1)}), bf16[192,896]{1,0:T(8,128)(2,1)}) %reduce-scatter.3.cloned.1.call-update) | async-done | bytes 344080 | tf_op jit(solution)/shard_map/reduce_scatter | solution.py:553
  402.9 3.5 all-to-all-start.1
  410.8 3.1 collective-permute-start.16
  414.5 15.6 %collective-permute-done.16 = bf16[96,1536]{1,0:T(8,128)(2,1)S(1)} collective-permute-done((bf16[96,1536]{1,0:T(8,128)(2,1)S(1)}, bf16[96,1536]{1,0:T(8,128)(2,1)S(1)}, u32[]{:S(2)}, u32[]{:S(2)}) %collective-permute-start.16) | collective-permute-done | bytes 294944 | tf_op jit(solution)/shard_map/ppermute | solution.py:536
  (217 shorter events, 53.7 us)
Async XLA Ops:
  7.2 88.5 %all-gather.4.cloned.1.call-start = ((), (), s32[]{:S(2)}) async-start(), calls=%async_computation.4 | async-start | bytes 3096576 | tf_op jit(solution)/shard_map/all_gather | solution.py:451
  8.7 15.0 %copy-start = (bf16[1,256,1536]{2,1,0:T(8,128)(2,1)S(1)}, bf16[1,256,1536]{2,1,0:T(8,128)(2,1)}, u32[]{:S(2)}) copy-start(bf16[1,256,1536]{2,1,0:T(8,128)(2,1)} %param.12) | copy-start | bytes 2359300
  8.9 15.0 %copy-start.21 = (f32[1536]{0:T(1024)S(1)}, f32[1536]{0:T(1024)}, u32[]{:S(2)}) copy-start(f32[1536]{0:T(1024)} %param.15) | copy-start | bytes 18436
  23.6 152.8 %all-gather.6.cloned.1.call-start = ((), (), s32[]{:S(2)}) async-start(), calls=%async_computation.5 | async-start | bytes 5308416 | tf_op jit(solution)/shard_map/all_gather | solution.py:462
  23.9 24.4 %copy-start.26 = (f32[256]{0:T(256)}, f32[256]{0:T(256)S(1)}, u32[]{:S(2)}) copy-start(f32[256]{0:T(256)S(1)} %fusion.15) | copy-start | bytes 3076
  23.9 24.4 %copy-start.24 = (f32[256]{0:T(256)}, f32[256]{0:T(256)S(1)}, u32[]{:S(2)}) copy-start(f32[256]{0:T(256)S(1)} %add_rsqrt_fusion) | copy-start | bytes 3076
  24.2 2.5 collective-permute-start
  28.5 20.7 %copy-start.5 = (bf16[512,1536]{1,0:T(8,128)(2,1)}, bf16[512,1536]{1,0:T(8,128)(2,1)S(1)}, u32[]{:S(2)}) copy-start(bf16[512,1536]{1,0:T(8,128)(2,1)S(1)} %maximum_select_fusion.2) | copy-start | bytes 4718596
  28.5 40.7 %collective-permute-start.1 = (bf16[512,1536]{1,0:T(8,128)(2,1)S(1)}, bf16[512,1536]{1,0:T(8,128)(2,1)}, u32[]{:S(2)}, u32[]{:S(2)}) collective-permute-start(bf16[512,1536]{1,0:T(8,128)(2,1)S(1)} %maximum_select_fusion.2), channel_id=1, source_target_pairs={{0,2},{1,3},{2,0},{3,1},{4,6},{5,7},{6,4},{7,5},{8,10},{9,11},{10,... | collective-permute-start | bytes 4718600 | tf_op jit(solution)/shard_map/ppermute | solution.py:360
  30.2 18.0 %collective-permute-start.2 = (bf16[96,1536]{1,0:T(8,128)(2,1)S(1)}, bf16[96,1536]{1,0:T(8,128)(2,1)S(1)}, u32[]{:S(2)}, u32[]{:S(2)}) collective-permute-start(bf16[96,1536]{1,0:T(8,128)(2,1)S(1)} %convert_element_type.173), channel_id=1, source_target_pairs={{0,0},{1,4},{2,8},{3,12},{4,16},{5,20},{6,24},{7,28},{8,1},{9,5},{... | collective-permute-start | bytes 884744 | tf_op jit(solution)/shard_map/ppermute | solution.py:454
  49.2 23.5 %copy-start.33 = (s32[1,256]{1,0:T(1,128)S(1)}, s32[1,256]{1,0:T(1,128)}, u32[]{:S(2)}) copy-start(s32[1,256]{1,0:T(1,128)} %param.13) | copy-start | bytes 3076
  49.2 29.5 %copy-start.34 = (f32[48]{0:T(128)S(1)}, f32[48]{0:T(128)}, u32[]{:S(2)}) copy-start(f32[48]{0:T(128)} %param.20) | copy-start | bytes 580
  49.2 29.5 %copy-start.35 = (f32[48]{0:T(128)S(1)}, f32[48]{0:T(128)}, u32[]{:S(2)}) copy-start(f32[48]{0:T(128)} %param.19) | copy-start | bytes 580
  49.2 29.6 %slice-start.3 = ((f32[3328]{0:T(1024)}), f32[3072]{0:T(1024)S(1)}, s32[]{:S(2)}) async-start(f32[3328]{0:T(1024)} %param.18), calls=%async_computation.11 | async-start | bytes 24576 | tf_op jit(solution)/shard_map/slice | solution.py:480
  49.2 31.2 %copy-start.37 = (f32[48]{0:T(128)S(1)}, f32[48]{0:T(128)}, u32[]{:S(2)}) copy-start(f32[48]{0:T(128)} %param.21) | copy-start | bytes 580
  49.2 32.8 %slice-start.2 = ((f32[3328]{0:T(1024)}), f32[256]{0:T(256)S(1)}, s32[]{:S(2)}) async-start(f32[3328]{0:T(1024)} %param.18), calls=%async_computation.10 | async-start | bytes 2048 | tf_op jit(solution)/shard_map/slice | solution.py:482
  49.3 32.9 %slice-start = ((f32[4,3328]{1,0:T(4,128)}), f32[4,256]{1,0:T(4,128)S(1)}, s32[]{:S(2)}) async-start(f32[4,3328]{1,0:T(4,128)} %param.17), calls=%async_computation.8 | async-start | bytes 8192 | tf_op jit(solution)/shard_map/slice | solution.py:481
  49.3 33.0 %slice-start.1 = ((f32[4,3328]{1,0:T(4,128)}), f32[4,3072]{1,0:T(4,128)S(1)}, s32[]{:S(2)}) async-start(f32[4,3328]{1,0:T(4,128)} %param.17), calls=%async_computation.9 | async-start | bytes 98304 | tf_op jit(solution)/shard_map/slice | solution.py:479
  72.6 285.0 %reduce-scatter.5.cloned.1.call-start = ((), (), s32[]{:S(2)}) async-start(), calls=%async_computation.7 | async-start | bytes 5308416 | tf_op jit(solution)/shard_map/reduce_scatter | solution.py:533
  72.6 10.3 %collective-permute-start.3 = (bf16[256,1536]{1,0:T(8,128)(2,1)}, bf16[256,1536]{1,0:T(8,128)(2,1)}, u32[]{:S(2)}, u32[]{:S(2)}) collective-permute-start(bf16[256,1536]{1,0:T(8,128)(2,1)} %bitcast.202), channel_id=1, source_target_pairs={{0,1},{1,0},{2,3},{3,2},{4,5},{5,4},{6,7},{7,6},{8,9},{9,8},{10,11... | collective-permute-start | bytes 2359304 | tf_op jit(solution)/shard_map/ppermute | solution.py:360
  86.4 98.2 %collective-permute-start.4 = (bf16[512,1536]{1,0:T(8,128)(2,1)}, bf16[512,1536]{1,0:T(8,128)(2,1)}, u32[]{:S(2)}, u32[]{:S(2)}) collective-permute-start(bf16[512,1536]{1,0:T(8,128)(2,1)} %maximum_select_fusion.3), channel_id=1, source_target_pairs={{0,2},{1,3},{2,0},{3,1},{4,6},{5,7},{6,4},{7,5},{8,10},{9,11},{10,... | collective-permute-start | bytes 4718600 | tf_op jit(solution)/shard_map/ppermute | solution.py:360
  184.6 9.6 %copy-start.9 = (f32[1024,768]{1,0:T(8,128)}, f32[1024,768]{1,0:T(8,128)S(1)}, u32[]{:S(2)}) copy-start(f32[1024,768]{1,0:T(8,128)S(1)} %fusion.62) | copy-start | bytes 9437188
  231.1 169.9 %reduce-scatter.3.cloned.1.call-start = ((), (), s32[]{:S(2)}) async-start(), calls=%async_computation.6 | async-start | bytes 3096576 | tf_op jit(solution)/shard_map/reduce_scatter | solution.py:553
  262.1 9.9 %copy-start.18 = (f32[1024,64]{0,1:T(8,128)S(1)}, f32[1024,64]{0,1:T(8,128)}, u32[]{:S(2)}) copy-start(f32[1024,64]{0,1:T(8,128)} %get-tuple-element.49) | copy-start | bytes 786436
  263.4 1.6 collective-permute-start.7
  266.3 5.6 %collective-permute-start.8 = (bf16[1,64,1024]{2,1,0:T(8,128)(2,1)S(1)}, bf16[1,64,1024]{2,1,0:T(8,128)(2,1)S(1)}, u32[]{:S(2)}, u32[]{:S(2)}) collective-permute-start(bf16[1,64,1024]{2,1,0:T(8,128)(2,1)S(1)} %fusion.37), channel_id=1, source_target_pairs={{0,2},{1,3},{2,0},{3,1},{4,6},{5,7},{6,4},{7,5},{8,10},{9,11},{10,... | collective-permute-start | bytes 393224 | tf_op jit(solution)/shard_map/ppermute | solution.py:360
  285.3 13.7 %collective-permute-start.9 = (bf16[2,256,1536]{2,1,0:T(8,128)(2,1)}, bf16[2,256,1536]{2,1,0:T(8,128)(2,1)}, u32[]{:S(2)}, u32[]{:S(2)}) collective-permute-start(bf16[2,256,1536]{2,1,0:T(8,128)(2,1)} %select_bitcast_fusion), channel_id=1, source_target_pairs={{0,1},{1,0},{2,3},{3,2},{4,5},{5,4},{6,7},{7,6},{8,9},{9,8},{10,11... | collective-permute-start | bytes 4718600 | tf_op jit(solution)/shard_map/ppermute | solution.py:360
  293.7 37.7 %collective-permute-start.5 = (bf16[2,256,1536]{2,1,0:T(8,128)(2,1)}, bf16[2,256,1536]{2,1,0:T(8,128)(2,1)}, u32[]{:S(2)}, u32[]{:S(2)}) collective-permute-start(bf16[2,256,1536]{2,1,0:T(8,128)(2,1)} %select_bitcast_fusion.1), channel_id=1, source_target_pairs={{0,1},{1,0},{2,3},{3,2},{4,5},{5,4},{6,7},{7,6},{8,9},{9,8},{10,11... | collective-permute-start | bytes 4718600 | tf_op jit(solution)/shard_map/ppermute | solution.py:360
  299.0 6.8 %copy-start.28 = (f32[64]{0:T(128)S(1)}, f32[64]{0:T(128)}, u32[]{:S(2)}) copy-start(f32[64]{0:T(128)} %get-tuple-element.39) | copy-start | bytes 772
  299.0 6.8 %copy-start.29 = (f32[64]{0:T(128)S(1)}, f32[64]{0:T(128)}, u32[]{:S(2)}) copy-start(f32[64]{0:T(128)} %get-tuple-element.40) | copy-start | bytes 772
  299.0 6.8 %copy-start.30 = (f32[64]{0:T(128)S(1)}, f32[64]{0:T(128)}, u32[]{:S(2)}) copy-start(f32[64]{0:T(128)} %get-tuple-element.41) | copy-start | bytes 772
  299.0 6.8 %copy-start.31 = (f32[64]{0:T(128)S(1)}, f32[64]{0:T(128)}, u32[]{:S(2)}) copy-start(f32[64]{0:T(128)} %get-tuple-element.37) | copy-start | bytes 772
  299.1 6.8 %copy-start.32 = (f32[64]{0:T(128)S(1)}, f32[64]{0:T(128)}, u32[]{:S(2)}) copy-start(f32[64]{0:T(128)} %get-tuple-element.38) | copy-start | bytes 772
  299.1 24.3 %copy-start.25 = (f32[256]{0:T(256)S(1)}, f32[256]{0:T(256)}, u32[]{:S(2)}) copy-start(f32[256]{0:T(256)} %copy-done.24) | copy-start | bytes 3076
  303.1 20.2 %collective-permute-start.10 = (bf16[1,256,1536]{2,1,0:T(8,128)(2,1)}, bf16[1,256,1536]{2,1,0:T(8,128)(2,1)}, u32[]{:S(2)}, u32[]{:S(2)}) collective-permute-start(bf16[1,256,1536]{2,1,0:T(8,128)(2,1)} %fusion.22), channel_id=1, source_target_pairs={{0,2},{1,3},{2,0},{3,1},{4,6},{5,7},{6,4},{7,5},{8,10},{9,11},{10,... | collective-permute-start | bytes 2359304 | tf_op jit(solution)/shard_map/ppermute | solution.py:360
  306.0 20.5 %copy-start.23 = (f32[768]{0:T(1024)S(1)}, f32[768]{0:T(1024)}, u32[]{:S(2)}) copy-start(f32[768]{0:T(1024)} %get-tuple-element.52) | copy-start | bytes 9220
  326.5 3.9 collective-permute-start.11
  330.4 9.2 %copy-start.27 = (f32[256]{0:T(256)S(1)}, f32[256]{0:T(256)}, u32[]{:S(2)}) copy-start(f32[256]{0:T(256)} %copy-done.26) | copy-start | bytes 3076
  330.4 4.1 collective-permute-start.12
  331.4 23.8 %copy-start.10 = (bf16[1,256,1536]{2,1,0:T(8,128)(2,1)S(1)}, bf16[1,256,1536]{2,1,0:T(8,128)(2,1)}, u32[]{:S(2)}) copy-start(bf16[1,256,1536]{2,1,0:T(8,128)(2,1)} %param.14) | copy-start | bytes 2359300
  334.5 20.8 %copy-start.1 = (bf16[1,256,1536]{2,1,0:T(8,128)(2,1)S(1)}, bf16[1,256,1536]{2,1,0:T(8,128)(2,1)}, u32[]{:S(2)}) copy-start(bf16[1,256,1536]{2,1,0:T(8,128)(2,1)} %param.12) | copy-start | bytes 2359300
  334.5 20.8 %copy-start.4 = (f32[1,256,1536]{2,1,0:T(8,128)S(1)}, f32[1,256,1536]{2,1,0:T(8,128)}, u32[]{:S(2)}) copy-start(f32[1,256,1536]{2,1,0:T(8,128)} %get-tuple-element.46) | copy-start | bytes 4718596
  334.5 4.9 %collective-permute-start.13 = (f32[6500]{0:T(1024)S(1)}, f32[6500]{0:T(1024)S(1)}, u32[]{:S(2)}, u32[]{:S(2)}) collective-permute-start(f32[6500]{0:T(1024)S(1)} %add.175), channel_id=1, source_target_pairs={{0,16},{4,20},{8,24},{12,28},{16,0},{20,4},{24,8},{28,12},{1,17},{... | collective-permute-start | bytes 78008 | tf_op jit(solution)/shard_map/ppermute | solution.py:400
  337.3 18.0 %collective-permute-start.6 = (bf16[1,256,1536]{2,1,0:T(8,128)(2,1)S(1)}, bf16[1,256,1536]{2,1,0:T(8,128)(2,1)S(1)}, u32[]{:S(2)}, u32[]{:S(2)}) collective-permute-start(bf16[1,256,1536]{2,1,0:T(8,128)(2,1)S(1)} %fusion.21), channel_id=1, source_target_pairs={{0,2},{1,3},{2,0},{3,1},{4,6},{5,7},{6,4},{7,5},{8,10},{9,11},{10,... | collective-permute-start | bytes 2359304 | tf_op jit(solution)/shard_map/ppermute | solution.py:360
  339.5 1.3 collective-permute-start.14
  340.8 16.6 %collective-permute-start.15 = (f32[2,6500]{1,0:T(2,128)S(1)}, f32[2,6500]{1,0:T(2,128)S(1)}, u32[]{:S(2)}, u32[]{:S(2)}) collective-permute-start(f32[2,6500]{1,0:T(2,128)S(1)} %maximum_select_fusion.7), channel_id=1, source_target_pairs={{0,2},{1,3},{2,0},{3,1},{4,6},{5,7},{6,4},{7,5},{8,10},{9,11},{10,... | collective-permute-start | bytes 156008 | tf_op jit(solution)/shard_map/ppermute | solution.py:360
  402.9 28.1 %all-to-all-start.1 = ((bf16[4,48,1664]{2,1,0:T(8,128)(2,1)}), bf16[4,48,1664]{2,1,0:T(8,128)(2,1)S(1)}, u32[]{:S(2)}, u32[]{:S(2)}) async-start(bf16[4,48,1664]{2,1,0:T(8,128)(2,1)} %bitcast.54), calls=%async_computation.3 | async-start | bytes 1277952 | tf_op jit(solution)/shard_map/all_to_all | solution.py:558
  410.8 19.3 %collective-permute-start.16 = (bf16[96,1536]{1,0:T(8,128)(2,1)S(1)}, bf16[96,1536]{1,0:T(8,128)(2,1)S(1)}, u32[]{:S(2)}, u32[]{:S(2)}) collective-permute-start(bf16[96,1536]{1,0:T(8,128)(2,1)S(1)} %bitcast.222), channel_id=1, source_target_pairs={{0,0},{4,1},{8,2},{12,3},{16,4},{20,5},{24,6},{28,7},{1,8},{5,9},{... | collective-permute-start | bytes 884744 | tf_op jit(solution)/shard_map/ppermute | solution.py:536
  (16 other events, 62.1 us)
Sparse Core Ops, SparseCore 0:
  23.7 71.9 all-gather.3
  98.5 77.9 all-gather.5
  231.3 95.3 reduce-scatter.4
  330.0 70.9 reduce-scatter.2

commit v3 on v2

--- a/solution.py
+++ b/solution.py
@@ -370,16 +370,18 @@
 
 def gathered(block):
     index = lax.axis_index("seq")
-    for bit in bits_of(lax.axis_size("seq")):
+    block = block[None]
+    for bit in reversed(bits_of(lax.axis_size("seq"))):
         other = swapped(block, bit)
         upper = (index & bit) != 0
         block = jnp.where(
-            upper, jnp.concatenate([other, block], axis=0), jnp.concatenate([block, other], axis=0)
+            upper, jnp.stack([other, block], axis=1), jnp.stack([block, other], axis=1)
         )
-    return block
-
-
-def scattered(parts):
+        block = block.reshape((-1,) + block.shape[2:])
+    return block.reshape((-1,) + block.shape[2:])
+
+
+def scattered(parts, between=lambda held: held):
     index = lax.axis_index("seq")
     size = lax.axis_size("seq")
     rest = parts.shape[1:]
@@ -390,7 +392,7 @@
         upper = (index & bit) != 0
         mine = jnp.where(upper, half[:, 1], half[:, 0])
         theirs = jnp.where(upper, half[:, 0], half[:, 1]).astype(bf16)
-        held = mine.astype(f32) + swapped(theirs, bit).astype(f32)
+        held = between(mine.astype(f32) + swapped(theirs, bit).astype(f32))
     return held[0]
 
 
@@ -399,6 +401,101 @@
     for bit in bits_of(count):
         block = block + lax.ppermute(block, "dp", [(i, i ^ bit) for i in range(count)])
     return block
+
+
+def moved_by(block, step):
+    count = lax.axis_size("dp")
+    route = [(i, i + 2 * step) for i in range(count) if 0 <= i + 2 * step < count]
+    return lax.ppermute(block, "dp", route)
+
+
+def crossed(block, bits):
+    return lax.ppermute(block, "dp", [(i, i ^ bits) for i in range(lax.axis_size("dp"))])
+
+
+def gathered_rows(block):
+    count = lax.axis_size("dp")
+    length = count // 2
+    if not is_small(count):
+        return lax.all_gather(block, "dp", axis=0, tiled=True)
+    at = lax.axis_index("dp")
+    place, side = at // 2, at % 2
+    rows = block.shape[0]
+    whole_rows = jnp.zeros((count * rows, block.shape[1]), block.dtype)
+
+    def put(into, piece, pair, half):
+        return lax.dynamic_update_slice(into, piece, ((pair * 2 + half) * rows, 0))
+
+    whole_rows = put(whole_rows, block, place, side)
+    whole_rows = put(whole_rows, crossed(block, 1), place, 1 - side)
+    up, down, ready = block, block, []
+    both = jnp.minimum(place, length - 1 - place)
+    for hop in range(1, length):
+        up, down = moved_by(up, 1), moved_by(down, -1)
+        ready.append((down, up))
+        piece, pair = None, None
+        for spot in range(length):
+            near = min(spot, length - 1 - spot)
+            if hop <= 2 * near:
+                away, from_below = (hop + 1) // 2, hop % 2 == 0
+            else:
+                away, from_below = hop - near, spot > length - 1 - spot
+            chosen = ready[away - 1][1 if from_below else 0]
+            source = spot - away if from_below else spot + away
+            here = place == spot
+            piece = chosen if piece is None else jnp.where(here, chosen, piece)
+            pair = source if pair is None else jnp.where(here, source, pair)
+        whole_rows = put(whole_rows, piece, pair, side)
+        whole_rows = put(whole_rows, crossed(piece, 1), pair, 1 - side)
+    return whole_rows
+
+
+def is_small(count):
+    return count <= 8 and count & (count - 1) == 0
+
+
+def halved_rows(term):
+    count = lax.axis_size("dp")
+    if not is_small(count):
+        return term
+    at = lax.axis_index("dp")
+    pairs = term.reshape(count // 2, 2, -1, term.shape[1])
+
+    def side(which):
+        return lax.dynamic_index_in_dim(pairs, which, 1, keepdims=False)
+
+    came = crossed(side((at & 1) ^ 1), 1)
+    return (side(at & 1).astype(f32) + came.astype(f32)).astype(bf16)
+
+
+def finished_rows(lines):
+    count = lax.axis_size("dp")
+    if not is_small(count):
+        return lax.psum_scatter(lines, "dp", scatter_dimension=0, tiled=True)
+    at = lax.axis_index("dp")
+
+    def part(owner):
+        return lax.dynamic_index_in_dim(lines, owner // 2, 0, keepdims=False)
+
+    came = [crossed(part(at ^ bits), bits) for bits in range(2, count, 2)]
+    return sum([piece.astype(f32) for piece in came], part(at).astype(f32)).astype(bf16)
+
+
+def after(value, other):
+    return lax.optimization_barrier((value, other))[0]
+
+
+def turned(blocks):
+    size = lax.axis_size("seq")
+    index = lax.axis_index("seq")
+    if size & (size - 1):
+        return lax.all_to_all(blocks, "seq", 0, 0, tiled=True)
+    out = blocks
+    for bits in range(1, size):
+        piece = lax.dynamic_slice_in_dim(blocks, index ^ bits, 1, 0)
+        piece = lax.ppermute(piece, "seq", [(i, i ^ bits) for i in range(size)])
+        out = lax.dynamic_update_slice_in_dim(out, piece, index ^ bits, 0)
+    return out
 
 
 def folded(rows, lead, width):
@@ -446,19 +543,20 @@
     gap = jnp.zeros((in_rows, size, LANES - own_heads - own_bc), bf16)
     laid = jnp.concatenate([x_cols, dt_cols, gap, bc_cols, z_cols], axis=2).transpose(1, 0, 2)
     mine = lax.all_to_all(laid, "seq", 0, 0, tiled=True)
+    flat = hidden.reshape(block, n_width).astype(f32)
+    inv = lax.rsqrt(jnp.mean(flat * flat, axis=-1, keepdims=True) + epsilon)
+    unit = flat * inv
+    normed_own = (unit * norm_gain).astype(bf16)
+    mine, normed_own = lax.optimization_barrier((mine, normed_own))
     mine = mine.reshape(size * in_rows, -1)
     n_first = own_inner + LANES
-    w_first = lax.all_gather(mine[:, :n_first], "dp", axis=0, tiled=True)
+    w_first = gathered_rows(mine[:, :n_first])
     order = [(f, (f % groups) * size + f // groups) for f in range(groups * size)]
     back = [(b, a) for a, b in order]
     out_moved = lax.ppermute(out_weight.astype(bf16), ("dp", "seq"), order)
     z_block = jnp.concatenate([mine[:, n_first:], folded(out_moved, 1, own_inner)], axis=0)
 
-    flat = hidden.reshape(block, n_width).astype(f32)
-    inv = lax.rsqrt(jnp.mean(flat * flat, axis=-1, keepdims=True) + epsilon)
-    unit = flat * inv
-    normed = gathered((unit * norm_gain).astype(bf16))
-    normed, z_block = lax.optimization_barrier((normed, z_block))
+    normed = gathered(normed_own)
     joined = lax.all_gather(z_block, "dp", axis=0, tiled=True).reshape(groups, -1, own_inner)
     z_rows = size * in_rows
     w_z = joined[:, :z_rows].reshape(-1, own_inner)
@@ -503,7 +601,7 @@
     for lag in range(1, n_taps):
         bc_conv = bc_conv + conv_bc[lag : lag + 1] * earlier(bc_in, lag) * same[lag]
     bc_sig = jax.nn.sigmoid(bc_conv)
-    bct = lax.all_gather((bc_conv * bc_sig).astype(bf16).T, "seq", axis=0, tiled=True)
+    bct = gathered((bc_conv * bc_sig).astype(bf16).T)
 
     y, states = run_forward(
         q, x_in, small_dt, bct, dcol, drow, conv_x, bias_x, sb, rate, skip, head
@@ -524,16 +622,13 @@
     d_z = (d_gated * y * (z_sig * (1.0 + z * (1.0 - z_sig)))).astype(bf16)
     d_y = d_gated * z_act
 
-    branch = scattered(mm(gate_low, w_out, NN).astype(bf16))
-    result = (flat + branch).reshape(n_seqs, block, n_width).astype(bf16)
-    out_term = mm(gate_low, cot, TN).astype(bf16)
-    z_term = mm(normed, d_z, TN).astype(bf16).reshape(groups, z_rows, own_inner)
-    terms = jnp.concatenate([z_term, folded(out_term, groups, own_inner)], axis=1)
-    terms, d_y = lax.optimization_barrier((terms.reshape(-1, own_inner), d_y))
+    terms = [mm(normed, d_z, TN)]
+    for k in range(0, n_width, own_inner):
+        terms.append(mm(gate_low, cot[:, k : k + own_inner], TN))
+    terms = [term.astype(bf16).reshape(groups, -1, own_inner) for term in terms]
+    terms = jnp.concatenate(terms, axis=1).reshape(-1, own_inner)
+    terms, d_y = lax.optimization_barrier((terms, d_y))
     parts = lax.psum_scatter(terms, "dp", scatter_dimension=0, tiled=True)
-    z_part = parts[:z_rows]
-    out_part = unfolded(parts[None, z_rows:], n_width)
-    d_out_weight = lax.ppermute(out_part, ("dp", "seq"), back).astype(f32)
 
     d_x, d_dt, d_bct, d_conv_x, d_heads = run_backward(
         q, x_in, small_dt, bct, dcol, drow, conv_x, bias_x, sb, rate, skip, d_y, states, head
@@ -550,18 +645,30 @@
     d_small = jnp.concatenate([d_dt[:, : LANES - own_bc], d_bc_in], axis=1).astype(bf16)
     d_first = jnp.concatenate([d_x, d_small], axis=1)
     first_term = mm(normed, d_first, TN).astype(bf16)
-    first_part = lax.psum_scatter(first_term, "dp", scatter_dimension=0, tiled=True)
-    d_normed = mm(d_first, w_first, NT) + mm(d_z, w_z, NT)
-    d_norm = scattered(d_normed.astype(bf16))
-
-    term = jnp.concatenate([first_part, z_part], axis=1).reshape(size, in_rows, -1)
-    moved = lax.all_to_all(term, "seq", 0, 0, tiled=True).transpose(1, 0, 2).astype(f32)
+    first_term, d_first = lax.optimization_barrier((first_term, d_first))
+    d_normed = (mm(d_first, w_first, NT) + mm(d_z, w_z, NT)).astype(bf16)
+    lines = after(halved_rows(first_term), d_normed)
+    first_part = finished_rows(lines)
+    d_norm = scattered(d_normed, lambda held: after(held, lines))
+    parts = after(parts, lines)
+    branch = after(mm(gate_low, w_out, NN).astype(bf16), parts)
+    branch = lax.psum_scatter(branch, "seq", scatter_dimension=0, tiled=True)
+    result = (flat + branch.astype(f32)).reshape(n_seqs, block, n_width).astype(bf16)
+
+    def own_rows(part):
+        out = turned(part.reshape(size, in_rows, -1))
+        return out.transpose(1, 0, 2).astype(f32)
+
+    out_part = unfolded(parts[None, z_rows:], n_width)
+    d_out_weight = lax.ppermute(out_part, ("dp", "seq"), back).astype(f32)
+    in_z = own_rows(parts[:z_rows])
+    in_first = own_rows(first_part)
     d_in_weight = jnp.concatenate(
         [
-            moved[:, :, n_first:].reshape(in_rows, n_inner),
-            moved[:, :, :own_inner].reshape(in_rows, n_inner),
-            moved[:, :, n_first - own_bc : n_first].reshape(in_rows, 2 * n_state),
-            moved[:, :, own_inner : own_inner + own_heads].reshape(in_rows, n_heads),
+            in_z.reshape(in_rows, n_inner),
+            in_first[:, :, :own_inner].reshape(in_rows, n_inner),
+            in_first[:, :, n_first - own_bc :].reshape(in_rows, 2 * n_state),
+            in_first[:, :, own_inner : own_inner + own_heads].reshape(in_rows, n_heads),
         ],
         axis=1,
     )
@@ -585,7 +692,7 @@
             d_norm_gain,
         ]
     )
-    packed = gathered(summed(packed)[None])
+    packed = gathered(summed(after(packed, first_part))[None])
     at = 0
 
     def take(count):

time: 445 us -> 428 us (0.962)
  blocking collectives: 49.3 us -> 12.8 us
  starting transfers between devices: 24.9 us -> 52.2 us
  local copies, waits for them, and re-layouts: 36.2 us -> 53.4 us
  other arithmetic: 53.3 us -> 43.2 us
  matrix products: 48.9 us -> 39.6 us
  waiting for transfers between devices: 168 us -> 160 us
    ppermute x0 -> x20, waiting for transfers between devices: none -> 113 us  [the longest x8 58.4 us: crossed(): lax.ppermute(block, 'dp', [(i, i ^ bits) for i in range(lax.axis_size('dp...]
    reduce_scatter x1, waiting for transfers between devices: 42.4 us -> 0.01 us  [shards(): branch = lax.psum_scatter(branch, 'seq', scatter_dimension=0, tiled=True)]
    ppermute x12, waiting for transfers between devices: 58.1 us -> 21.4 us  [swapped(): return lax.ppermute(block, 'seq', [(i, i ^ bit) for i in range(size)])]
    ppermute x0 -> x20, starting transfers between devices: none -> 27 us  [the longest x6 17.5 us: moved_by(): return lax.ppermute(block, 'dp', route)]
    all_gather x1, waiting for transfers between devices: 26.8 us -> 0.01 us  [shards(): lax.all_gather(z_block, 'dp', axis=0, tiled=True)]
    all_gather x1 -> x0, blocking collectives: 24.7 us -> none  [shards(): lax.all_gather((bc_conv * bc_sig).astype(bf16).T, 'seq', axis=0, tiled=True)]
    all_to_all x1 -> x0, blocking collectives: 12.6 us -> none  [shards(): mine = lax.all_to_all(laid, 'seq', 0, 0, tiled=True)]
    dot_general x10 -> x11, matrix products: 48.9 us -> 39.6 us  [mm(): return lax.dot_general(a, b, (dims, ((), ())), preferred_element_type=out)]
  transfers between devices with their start and end apart: 22 -> 41, of which waited for: 14 -> 23; matrix products, arithmetic and copies ran while one was open for 20% -> 21% of each run, Pallas kernels for 10% -> 11%
where the time goes in v3:
time: 428 us; the launch traced here: 421 us
  waiting for transfers between devices  160 us (37%)
  local copies, waits for them, and re-layouts  53.4 us (12%)
  starting transfers between devices  52.2 us (12%)
  Pallas kernels  44.3 us (10%)
  other arithmetic  43.2 us (10%)
  matrix products  39.6 us (9%)
  between operations  15.2 us (4%)
  blocking collectives  12.8 us (3%)
    ppermute x8, waiting for transfers between devices, crossed(): lax.ppermute(block, 'dp', [(i, i ^ bits) for i in range(lax.axis_size('dp...  58.4 us
    ppermute x6, waiting for transfers between devices, moved_by(): return lax.ppermute(block, 'dp', route)  50.7 us
    dot_general x11, matrix products, mm(): return lax.dot_general(a, b, (dims, ((), ())), preferred_element_type=out)  39.6 us
    pallas_call x1, Pallas kernels, run_backward(): pl.pallas_call(functools.partial(scan_backward, q, taps, pairs, head, chu...  30.9 us
    ppermute x12, waiting for transfers between devices, swapped(): return lax.ppermute(block, 'seq', [(i, i ^ bit) for i in range(size)])  21.4 us
    ppermute x6, starting transfers between devices, moved_by(): return lax.ppermute(block, 'dp', route)  17.5 us
    ppermute x12, starting transfers between devices, swapped(): return lax.ppermute(block, 'seq', [(i, i ^ bit) for i in range(size)])  15.2 us
    unnamed x81, local copies, waits for them, and re-layouts  14.1 us
  transfers between devices with their start and end apart: 41, of which 23 were waited for; matrix products, arithmetic and copies ran while one was open for 21% of the time, Pallas kernels for 11%

profile of v3, /device:TPU:2, one launch (start us, length us, event | category | flops | bytes accessed | tf_op | source)
XLA Modules:
  0.0 421.1 jit_solution(12276141216772085000)
XLA Ops:
  10.9 3.5 all-to-all-start
  14.5 4.5 %collective-permute-start.14 = (bf16[96,1536]{1,0:T(8,128)(2,1)S(1)}, bf16[96,1536]{1,0:T(8,128)(2,1)S(1)}, u32[]{:S(2)}, u32[]{:S(2)}) collective-permute-start(bf16[96,1536]{1,0:T(8,128)(2,1)S(1)} %convert_element_type.190), channel_id=1, source_target_pairs={{0,0},{1,4},{2,8},{3,12},{4,16},{5,20},{6,24},{7,28},{8,1},{9,5},{... | collective-permute-start | bytes 884744 | tf_op jit(solution)/shard_map/ppermute | solution.py:556
  19.5 6.3 %collective-permute-done.14 = bf16[96,1536]{1,0:T(8,128)(2,1)S(1)} collective-permute-done((bf16[96,1536]{1,0:T(8,128)(2,1)S(1)}, bf16[96,1536]{1,0:T(8,128)(2,1)S(1)}, u32[]{:S(2)}, u32[]{:S(2)}) %collective-permute-start.14) | collective-permute-done | bytes 294944 | tf_op jit(solution)/shard_map/ppermute | solution.py:556
  29.6 10.2 %collective-permute-start.15 = (bf16[1,256,1536]{2,1,0:T(8,128)(2,1)S(1)}, bf16[1,256,1536]{2,1,0:T(8,128)(2,1)S(1)}, u32[]{:S(2)}, u32[]{:S(2)}) collective-permute-start(bf16[1,256,1536]{2,1,0:T(8,128)(2,1)S(1)} %copy-done.2), channel_id=1, source_target_pairs={{0,2},{1,3},{2,0},{3,1},{4,6},{5,7},{6,4},{7,5},{8,10},{9,11},{10,... | collective-permute-start | bytes 2359304 | tf_op jit(solution)/shard_map/ppermute | solution.py:360
  39.9 3.6 collective-permute-start.3
  49.1 4.5 %collective-permute-done.3 = bf16[192,896]{1,0:T(8,128)(2,1)S(1)} collective-permute-done((bf16[192,896]{1,0:T(8,128)(2,1)}, bf16[192,896]{1,0:T(8,128)(2,1)S(1)}, u32[]{:S(2)}, u32[]{:S(2)}) %collective-permute-start.3) | collective-permute-done | bytes 344096 | tf_op jit(solution)/shard_map/ppermute | solution.py:409
  53.6 17.6 %collective-permute-done.4 = bf16[192,896]{1,0:T(8,128)(2,1)S(1)} collective-permute-done((bf16[192,896]{1,0:T(8,128)(2,1)}, bf16[192,896]{1,0:T(8,128)(2,1)S(1)}, u32[]{:S(2)}, u32[]{:S(2)}) %collective-permute-start.4) | collective-permute-done | bytes 344096 | tf_op jit(solution)/shard_map/ppermute | solution.py:409
  72.9 3.2 collective-permute-start.5
  76.7 5.3 %all-gather = s32[1,1024]{1,0:T(1,128)S(1)} all-gather(s32[1,256]{1,0:T(1,128)} %param.13), channel_id=2, replica_groups=mesh['dp'=8,'seq'=4] {'seq'}, dimensions={1}, use_global_device_ids=true | all-gather | bytes 5120 | tf_op jit(solution)/shard_map/all_gather | solution.py:566
  88.2 5.3 %collective-permute-start.6 = (bf16[192,896]{1,0:T(8,128)(2,1)S(1)}, bf16[192,896]{1,0:T(8,128)(2,1)S(1)}, u32[]{:S(2)}, u32[]{:S(2)}) collective-permute-start(bf16[192,896]{1,0:T(8,128)(2,1)S(1)} %collective-permute-done.3), channel_id=1, source_target_pairs={{0,8},{4,12},{8,16},{12,20},{16,24},{20,28},{1,9},{5,13},{9,17},{1... | collective-permute-start | bytes 1032200 | tf_op jit(solution)/shard_map/ppermute | solution.py:409
  96.9 12.2 %collective-permute-done.6 = bf16[192,896]{1,0:T(8,128)(2,1)S(1)} collective-permute-done((bf16[192,896]{1,0:T(8,128)(2,1)S(1)}, bf16[192,896]{1,0:T(8,128)(2,1)S(1)}, u32[]{:S(2)}, u32[]{:S(2)}) %collective-permute-start.6) | collective-permute-done | bytes 344096 | tf_op jit(solution)/shard_map/ppermute | solution.py:409
  109.1 11.3 %collective-permute-done.7 = bf16[192,896]{1,0:T(8,128)(2,1)S(1)} collective-permute-done((bf16[192,896]{1,0:T(8,128)(2,1)}, bf16[192,896]{1,0:T(8,128)(2,1)S(1)}, u32[]{:S(2)}, u32[]{:S(2)}) %collective-permute-start.7) | collective-permute-done | bytes 344096 | tf_op jit(solution)/shard_map/ppermute | solution.py:409
  122.0 4.7 %collective-permute-start.9 = (bf16[192,896]{1,0:T(8,128)(2,1)S(1)}, bf16[192,896]{1,0:T(8,128)(2,1)S(1)}, u32[]{:S(2)}, u32[]{:S(2)}) collective-permute-start(bf16[192,896]{1,0:T(8,128)(2,1)S(1)} %collective-permute-done.6), channel_id=1, source_target_pairs={{0,8},{4,12},{8,16},{12,20},{16,24},{20,28},{1,9},{5,13},{9,17},{1... | collective-permute-start | bytes 1032200 | tf_op jit(solution)/shard_map/ppermute | solution.py:409
  127.0 3.2 collective-permute-done.8
  130.2 5.1 %collective-permute-done.10 = bf16[192,896]{1,0:T(8,128)(2,1)S(1)} collective-permute-done((bf16[192,896]{1,0:T(8,128)(2,1)S(1)}, bf16[192,896]{1,0:T(8,128)(2,1)S(1)}, u32[]{:S(2)}, u32[]{:S(2)}) %collective-permute-start.10) | collective-permute-done | bytes 344096 | tf_op jit(solution)/shard_map/ppermute | solution.py:409
  136.7 8.8 %collective-permute-done.11 = bf16[192,896]{1,0:T(8,128)(2,1)S(1)} collective-permute-done((bf16[192,896]{1,0:T(8,128)(2,1)S(1)}, bf16[192,896]{1,0:T(8,128)(2,1)S(1)}, u32[]{:S(2)}, u32[]{:S(2)}) %collective-permute-start.11) | collective-permute-done | bytes 344096 | tf_op jit(solution)/shard_map/ppermute | solution.py:413
  154.0 3.2 collective-permute-done.12
  157.5 3.7 fusion.10.x_ref.xp_ref
  162.6 2.3 copy.90
  166.6 13.5 %scan_forward.1 = (f32[1024,768]{1,0:T(8,128)}, f32[8,128,768]{2,1,0:T(8,128)}) custom-call(bf16[1024,768]{1,0:T(8,128)(2,1)} %fusion.10.x_ref.xp_ref, f32[1024,128]{1,0:T(8,128)} %get-tuple-element.110.small_ref, bf16[256,1024]{1,0:T(8,128)(2,1)} %bitcast.217, f32[1024,128]{1,0:T(8,128)} %broadcast_in_dim.71.dcol_ref.dcolp_ref, ...), custom_call_target="tpu_custom_call" | custom-call | tf_op jit(solution)/shard_map/scan_forward/pallas_call | solution.py:270
  180.1 2.7 fusion.66
  182.8 2.6 fusion.72
  185.4 2.4 copy.95
  188.5 2.3 copy-done.9
  190.8 5.3 %multiply_reduce_fusion.2 = (f32[1024]{0:T(1024)S(1)}, f32[1024]{0:T(1024)S(1)}, f32[1024,768]{1,0:T(8,128)}, f32[1024,768]{1,0:T(8,128)}) fusion(f32[768]{0:T(1024)S(1)} %dynamic-slice.23, f32[1024,768]{1,0:T(8,128)S(1)} %copy-done.11, f32[1024,768]{1,0:T(8,128)S(1)} %fusion.72, bf16[1024,1536]{1,0:T(8,128)(2,1)S(1)} %bitcast.220, ...), kind=kOutput, calls=%fused_computation.13 | convolution fusion | flops 2423781376 | bytes 18099200 | tf_op jit(solution)/shard_map/dot_general | solution.py:20
  196.0 7.5 %psum.7 = f32[2,1024]{1,0:T(2,128)S(1)} all-reduce(f32[2,1024]{1,0:T(2,128)S(1)} %pad_maximum_fusion.5), channel_id=1, replica_groups=mesh['dp'=8,'seq'=4] {'seq'}, use_global_device_ids=true, to_apply=%region_3.4 | all-reduce | flops 2048 | bytes 16384 | tf_op jit(solution)/shard_map/psum | solution.py:616
  203.6 7.8 %fusion.24 = (f32[1024,768]{1,0:T(8,128)}, bf16[1024,768]{1,0:T(8,128)(2,1)S(1)}, f32[768]{0:T(1024)}, bf16[1024,768]{1,0:T(8,128)(2,1)S(1)}) fusion(f32[1024,768]{1,0:T(8,128)} %get-tuple-element.62, f32[1024]{0:T(1024)S(1)} %fusion.53, f32[1024,768]{1,0:T(8,128)} %get-tuple-element.112, f32[1024]{0:T(1024)S(1)} %bitcast.265, f32[768]{0:T(1024)S(1)} %dynamic-slice.23, ...), kind=kLoop, calls=%fused_computation.51 | loop fusion | flops 17300736 | bytes 18888704 | tf_op jit(solution)/shard_map/mul | solution.py:623
  214.3 3.0 convolution_convert_fusion.2
  217.3 2.4 pad_maximum_fusion
  219.8 30.9 %scan_backward.1 = (bf16[1024,768]{1,0:T(8,128)(2,1)}, f32[1024,128]{1,0:T(8,128)}, f32[256,1024]{1,0:T(8,128)}, f32[8,768]{1,0:T(8,128)}, f32[8,128]{1,0:T(8,128)}) custom-call(bf16[1024,768]{1,0:T(8,128)(2,1)} %fusion.10.x_ref.xp_ref, bf16[1024,768]{1,0:T(8,128)(2,1)} %fusion.10.x_ref.xp_ref, f32[1024,128]{1,0:T(8,128)} %get-tuple-element.110.small_ref, ...), custom_call_target="tpu_custom_call" | custom-call | tf_op jit(solution)/shard_map/scan_backward/pallas_call | solution.py:315
  252.9 2.4 copy.111
  255.3 2.4 copy.112
  264.1 4.6 %fusion.73 = f32[1024,1536]{1,0:T(8,128)} fusion(bf16[1024,768]{1,0:T(8,128)(2,1)S(1)} %copy-done.26, bf16[1536,768]{1,0:T(8,128)(2,1)S(1)} %bitcast.240), kind=kOutput, calls=%fused_computation.182 | convolution fusion | flops 2415919104 | bytes 10223616 | tf_op jit(solution)/shard_map/dot_general | solution.py:20
  268.7 3.3 collective-permute-done.18
  275.8 3.7 convolution_convert_fusion.1
  282.5 4.3 %convolution_convert_fusion = bf16[1024,1536]{1,0:T(8,128)(2,1)} fusion(bf16[1024,768]{1,0:T(8,128)(2,1)S(1)} %copy-done.24, bf16[768,1536]{1,0:T(8,128)(2,1)S(1)} %bitcast.235), kind=kOutput, calls=%fused_computation.2 | convolution fusion | flops 2417491968 | bytes 7077888 | tf_op jit(solution)/shard_map/dot_general | solution.py:20
  286.9 7.8 %add_convert_fusion = bf16[1024,1536]{1,0:T(8,128)(2,1)S(1)} fusion(f32[1024,1536]{1,0:T(8,128)} %fusion.73, bf16[1024,896]{1,0:T(8,128)(2,1)} %copy-done.21, bf16[1536,896]{1,0:T(8,128)(2,1)} %copy-done.8), kind=kOutput, calls=%fused_computation | convolution fusion | flops 2821718016 | bytes 14024704 | tf_op jit(solution)/shard_map/dot_general | solution.py:20
  294.7 25.6 %collective-permute-done.19 = bf16[4,192,896]{2,1,0:T(8,128)(2,1)} collective-permute-done((bf16[4,192,896]{2,1,0:T(8,128)(2,1)}, bf16[4,192,896]{2,1,0:T(8,128)(2,1)}, u32[]{:S(2)}, u32[]{:S(2)}) %collective-permute-start.19) | collective-permute-done | bytes 1376288 | tf_op jit(solution)/shard_map/ppermute | solution.py:413
  320.2 2.8 fusion.1
  335.5 9.2 %collective-permute-done.22 = bf16[192,896]{1,0:T(8,128)(2,1)S(1)} collective-permute-done((bf16[192,896]{1,0:T(8,128)(2,1)S(1)}, bf16[192,896]{1,0:T(8,128)(2,1)S(1)}, u32[]{:S(2)}, u32[]{:S(2)}) %collective-permute-start.22) | collective-permute-done | bytes 344096 | tf_op jit(solution)/shard_map/ppermute | solution.py:413
  344.7 11.8 %collective-permute-done.23 = bf16[192,896]{1,0:T(8,128)(2,1)S(1)} collective-permute-done((bf16[192,896]{1,0:T(8,128)(2,1)S(1)}, bf16[192,896]{1,0:T(8,128)(2,1)S(1)}, u32[]{:S(2)}, u32[]{:S(2)}) %collective-permute-start.23) | collective-permute-done | bytes 344096 | tf_op jit(solution)/shard_map/ppermute | solution.py:413
  359.2 9.7 %collective-permute-done.21 = bf16[1,256,1536]{2,1,0:T(8,128)(2,1)S(1)} collective-permute-done((bf16[1,256,1536]{2,1,0:T(8,128)(2,1)S(1)}, bf16[1,256,1536]{2,1,0:T(8,128)(2,1)S(1)}, u32[]{:S(2)}, u32[]{:S(2)}) %collective-permute-start.21) | collective-permute-done | bytes 786464 | tf_op jit(solution)/shard_map/ppermute | solution.py:360
  371.7 3.9 collective-permute-done.32
  376.6 10.1 %collective-permute-done.36 = bf16[96,1536]{1,0:T(8,128)(2,1)S(1)} collective-permute-done((bf16[96,1536]{1,0:T(8,128)(2,1)S(1)}, bf16[96,1536]{1,0:T(8,128)(2,1)S(1)}, u32[]{:S(2)}, u32[]{:S(2)}) %collective-permute-start.36) | collective-permute-done | bytes 294944 | tf_op jit(solution)/shard_map/ppermute | solution.py:663
  387.6 3.1 fusion.14
  392.5 2.8 collective-permute-done.25
  396.0 3.2 collective-permute-done.26
  400.8 3.2 collective-permute-done.27
  (279 shorter events, 93.5 us)
Async XLA Ops:
  10.9 15.1 %all-to-all-start = ((bf16[4,48,1664]{2,1,0:T(8,128)(2,1)}), bf16[4,48,1664]{2,1,0:T(8,128)(2,1)S(1)}, u32[]{:S(2)}, u32[]{:S(2)}) async-start(bf16[4,48,1664]{2,1,0:T(8,128)(2,1)} %copy.85), calls=%async_computation | async-start | bytes 1277952 | tf_op jit(solution)/shard_map/all_to_all | solution.py:545
  14.4 165.7 %all-gather.3.cloned.1.call-start = ((), (), s32[]{:S(2)}) async-start(), calls=%async_computation.3 | async-start | bytes 5308416 | tf_op jit(solution)/shard_map/all_gather | solution.py:560
  14.5 11.4 %collective-permute-start.14 = (bf16[96,1536]{1,0:T(8,128)(2,1)S(1)}, bf16[96,1536]{1,0:T(8,128)(2,1)S(1)}, u32[]{:S(2)}, u32[]{:S(2)}) collective-permute-start(bf16[96,1536]{1,0:T(8,128)(2,1)S(1)} %convert_element_type.190), channel_id=1, source_target_pairs={{0,0},{1,4},{2,8},{3,12},{4,16},{5,20},{6,24},{7,28},{8,1},{9,5},{... | collective-permute-start | bytes 884744 | tf_op jit(solution)/shard_map/ppermute | solution.py:556
  26.9 12.9 %slice-start = ((f32[4,3328]{1,0:T(4,128)}), f32[4,256]{1,0:T(4,128)S(1)}, s32[]{:S(2)}) async-start(f32[4,3328]{1,0:T(4,128)} %param.17), calls=%async_computation.6 | async-start | bytes 8192 | tf_op jit(solution)/shard_map/slice | solution.py:579
  26.9 296.1 %reduce-scatter.3.cloned.1.call-start = ((), (), s32[]{:S(2)}) async-start(), calls=%async_computation.4 | async-start | bytes 5308416 | tf_op jit(solution)/shard_map/reduce_scatter | solution.py:631
  27.0 49.0 %slice-start.1 = ((f32[4,3328]{1,0:T(4,128)}), f32[4,3072]{1,0:T(4,128)S(1)}, s32[]{:S(2)}) async-start(f32[4,3328]{1,0:T(4,128)} %param.17), calls=%async_computation.7 | async-start | bytes 98304 | tf_op jit(solution)/shard_map/slice | solution.py:577
  29.6 17.8 %collective-permute-start.2 = (bf16[192,896]{1,0:T(8,128)(2,1)}, bf16[192,896]{1,0:T(8,128)(2,1)}, u32[]{:S(2)}, u32[]{:S(2)}) collective-permute-start(bf16[192,896]{1,0:T(8,128)(2,1)} %get-tuple-element.83), channel_id=1, source_target_pairs={{0,4},{4,0},{8,12},{12,8},{16,20},{20,16},{24,28},{28,24},{1,5},{5... | collective-permute-start | bytes 1032200 | tf_op jit(solution)/shard_map/ppermute | solution.py:413
  29.6 97.1 %collective-permute-start.15 = (bf16[1,256,1536]{2,1,0:T(8,128)(2,1)S(1)}, bf16[1,256,1536]{2,1,0:T(8,128)(2,1)S(1)}, u32[]{:S(2)}, u32[]{:S(2)}) collective-permute-start(bf16[1,256,1536]{2,1,0:T(8,128)(2,1)S(1)} %copy-done.2), channel_id=1, source_target_pairs={{0,2},{1,3},{2,0},{3,1},{4,6},{5,7},{6,4},{7,5},{8,10},{9,11},{10,... | collective-permute-start | bytes 2359304 | tf_op jit(solution)/shard_map/ppermute | solution.py:360
  39.9 13.7 %collective-permute-start.3 = (bf16[192,896]{1,0:T(8,128)(2,1)}, bf16[192,896]{1,0:T(8,128)(2,1)S(1)}, u32[]{:S(2)}, u32[]{:S(2)}) collective-permute-start(bf16[192,896]{1,0:T(8,128)(2,1)} %get-tuple-element.83), channel_id=1, source_target_pairs={{0,8},{4,12},{8,16},{12,20},{16,24},{20,28},{1,9},{5,13},{9,17},{1... | collective-permute-start | bytes 1032200 | tf_op jit(solution)/shard_map/ppermute | solution.py:409
  43.5 27.7 %collective-permute-start.4 = (bf16[192,896]{1,0:T(8,128)(2,1)}, bf16[192,896]{1,0:T(8,128)(2,1)S(1)}, u32[]{:S(2)}, u32[]{:S(2)}) collective-permute-start(bf16[192,896]{1,0:T(8,128)(2,1)} %get-tuple-element.83), channel_id=1, source_target_pairs={{8,0},{12,4},{16,8},{20,12},{24,16},{28,20},{9,1},{13,5},{17,9},{2... | collective-permute-start | bytes 1032200 | tf_op jit(solution)/shard_map/ppermute | solution.py:409
  45.3 51.2 %collective-permute-start = (bf16[1,256,1536]{2,1,0:T(8,128)(2,1)S(1)}, bf16[1,256,1536]{2,1,0:T(8,128)(2,1)S(1)}, u32[]{:S(2)}, u32[]{:S(2)}) collective-permute-start(bf16[1,256,1536]{2,1,0:T(8,128)(2,1)S(1)} %bitcast.213), channel_id=1, source_target_pairs={{0,2},{1,3},{2,0},{3,1},{4,6},{5,7},{6,4},{7,5},{8,10},{9,11},{10,... | collective-permute-start | bytes 2359304 | tf_op jit(solution)/shard_map/ppermute | solution.py:360
  72.9 21.9 %collective-permute-start.5 = (bf16[192,896]{1,0:T(8,128)(2,1)}, bf16[192,896]{1,0:T(8,128)(2,1)}, u32[]{:S(2)}, u32[]{:S(2)}) collective-permute-start(bf16[192,896]{1,0:T(8,128)(2,1)} %get-tuple-element.70), channel_id=1, source_target_pairs={{0,4},{4,0},{8,12},{12,8},{16,20},{20,16},{24,28},{28,24},{1,5},{5... | collective-permute-start | bytes 1032200 | tf_op jit(solution)/shard_map/ppermute | solution.py:413
  88.2 20.9 %collective-permute-start.6 = (bf16[192,896]{1,0:T(8,128)(2,1)S(1)}, bf16[192,896]{1,0:T(8,128)(2,1)S(1)}, u32[]{:S(2)}, u32[]{:S(2)}) collective-permute-start(bf16[192,896]{1,0:T(8,128)(2,1)S(1)} %collective-permute-done.3), channel_id=1, source_target_pairs={{0,8},{4,12},{8,16},{12,20},{16,24},{20,28},{1,9},{5,13},{9,17},{1... | collective-permute-start | bytes 1032200 | tf_op jit(solution)/shard_map/ppermute | solution.py:409
  93.5 26.9 %collective-permute-start.7 = (bf16[192,896]{1,0:T(8,128)(2,1)}, bf16[192,896]{1,0:T(8,128)(2,1)S(1)}, u32[]{:S(2)}, u32[]{:S(2)}) collective-permute-start(bf16[192,896]{1,0:T(8,128)(2,1)} %copy-done.29), channel_id=1, source_target_pairs={{8,0},{12,4},{16,8},{20,12},{24,16},{28,20},{9,1},{13,5},{17,9},{2... | collective-permute-start | bytes 1032200 | tf_op jit(solution)/shard_map/ppermute | solution.py:409
  96.5 23.9 %copy-start.7 = (bf16[1536,896]{1,0:T(8,128)(2,1)S(1)}, bf16[1536,896]{1,0:T(8,128)(2,1)}, u32[]{:S(2)}) copy-start(bf16[1536,896]{1,0:T(8,128)(2,1)} %constant_dynamic-update-slice_fusion.10) | copy-start | bytes 8257540
  96.8 48.8 %collective-permute-start.1 = (bf16[2,256,1536]{2,1,0:T(8,128)(2,1)S(1)}, bf16[2,256,1536]{2,1,0:T(8,128)(2,1)S(1)}, u32[]{:S(2)}, u32[]{:S(2)}) collective-permute-start(bf16[2,256,1536]{2,1,0:T(8,128)(2,1)S(1)} %maximum_select_fusion.2), channel_id=1, source_target_pairs={{0,1},{1,0},{2,3},{3,2},{4,5},{5,4},{6,7},{7,6},{8,9},{9,8},{10,11... | collective-permute-start | bytes 4718600 | tf_op jit(solution)/shard_map/ppermute | solution.py:360
  120.6 9.6 %collective-permute-start.8 = (bf16[192,896]{1,0:T(8,128)(2,1)S(1)}, bf16[192,896]{1,0:T(8,128)(2,1)S(1)}, u32[]{:S(2)}, u32[]{:S(2)}) collective-permute-start(bf16[192,896]{1,0:T(8,128)(2,1)S(1)} %get-tuple-element.68), channel_id=1, source_target_pairs={{0,4},{4,0},{8,12},{12,8},{16,20},{20,16},{24,28},{28,24},{1,5},{5... | collective-permute-start | bytes 1032200 | tf_op jit(solution)/shard_map/ppermute | solution.py:413
  120.7 14.7 %collective-permute-start.10 = (bf16[192,896]{1,0:T(8,128)(2,1)S(1)}, bf16[192,896]{1,0:T(8,128)(2,1)S(1)}, u32[]{:S(2)}, u32[]{:S(2)}) collective-permute-start(bf16[192,896]{1,0:T(8,128)(2,1)S(1)} %collective-permute-done.7), channel_id=1, source_target_pairs={{8,0},{12,4},{16,8},{20,12},{24,16},{28,20},{9,1},{13,5},{17,9},{2... | collective-permute-start | bytes 1032200 | tf_op jit(solution)/shard_map/ppermute | solution.py:409
  122.0 13.4 %collective-permute-start.9 = (bf16[192,896]{1,0:T(8,128)(2,1)S(1)}, bf16[192,896]{1,0:T(8,128)(2,1)S(1)}, u32[]{:S(2)}, u32[]{:S(2)}) collective-permute-start(bf16[192,896]{1,0:T(8,128)(2,1)S(1)} %collective-permute-done.6), channel_id=1, source_target_pairs={{0,8},{4,12},{8,16},{12,20},{16,24},{20,28},{1,9},{5,13},{9,17},{1... | collective-permute-start | bytes 1032200 | tf_op jit(solution)/shard_map/ppermute | solution.py:409
  127.0 24.6 %collective-permute-start.16 = (bf16[2,256,1536]{2,1,0:T(8,128)(2,1)S(1)}, bf16[2,256,1536]{2,1,0:T(8,128)(2,1)S(1)}, u32[]{:S(2)}, u32[]{:S(2)}) collective-permute-start(bf16[2,256,1536]{2,1,0:T(8,128)(2,1)S(1)} %maximum_select_fusion.3), channel_id=1, source_target_pairs={{0,1},{1,0},{2,3},{3,2},{4,5},{5,4},{6,7},{7,6},{8,9},{9,8},{10,11... | collective-permute-start | bytes 4718600 | tf_op jit(solution)/shard_map/ppermute | solution.py:360
  135.6 9.9 %collective-permute-start.11 = (bf16[192,896]{1,0:T(8,128)(2,1)S(1)}, bf16[192,896]{1,0:T(8,128)(2,1)S(1)}, u32[]{:S(2)}, u32[]{:S(2)}) collective-permute-start(bf16[192,896]{1,0:T(8,128)(2,1)S(1)} %get-tuple-element.66), channel_id=1, source_target_pairs={{0,4},{4,0},{8,12},{12,8},{16,20},{20,16},{24,28},{28,24},{1,5},{5... | collective-permute-start | bytes 1032200 | tf_op jit(solution)/shard_map/ppermute | solution.py:413
  145.5 11.9 %copy-start.8 = (bf16[1536,896]{1,0:T(8,128)(2,1)}, bf16[1536,896]{1,0:T(8,128)(2,1)S(1)}, u32[]{:S(2)}) copy-start(bf16[1536,896]{1,0:T(8,128)(2,1)S(1)} %constant_dynamic-update-slice_fusion.6) | copy-start | bytes 8257540
  150.0 7.2 %collective-permute-start.12 = (bf16[1,64,1024]{1,2,0:T(8,128)(2,1)S(1)}, bf16[1,64,1024]{1,2,0:T(8,128)(2,1)S(1)}, u32[]{:S(2)}, u32[]{:S(2)}) collective-permute-start(bf16[1,64,1024]{1,2,0:T(8,128)(2,1)S(1)} %bitcast.236), channel_id=1, source_target_pairs={{0,2},{1,3},{2,0},{3,1},{4,6},{5,7},{6,4},{7,5},{8,10},{9,11},{10,... | collective-permute-start | bytes 393224 | tf_op jit(solution)/shard_map/ppermute | solution.py:360
  157.4 3.9 collective-permute-start.13
  219.7 167.8 %reduce-scatter.5.cloned.1.call-start = ((), (), s32[]{:S(2)}) async-start(), calls=%async_computation.5 | async-start | bytes 3932160 | tf_op jit(solution)/shard_map/reduce_scatter | solution.py:655
  259.8 2.3 collective-permute-start.17
  263.7 8.4 %collective-permute-start.18 = (bf16[1,64,1024]{1,2,0:T(8,128)(2,1)S(1)}, bf16[1,64,1024]{1,2,0:T(8,128)(2,1)S(1)}, u32[]{:S(2)}, u32[]{:S(2)}) collective-permute-start(bf16[1,64,1024]{1,2,0:T(8,128)(2,1)S(1)} %fusion.49), channel_id=1, source_target_pairs={{0,2},{1,3},{2,0},{3,1},{4,6},{5,7},{6,4},{7,5},{8,10},{9,11},{10,... | collective-permute-start | bytes 393224 | tf_op jit(solution)/shard_map/ppermute | solution.py:360
  282.2 38.0 %collective-permute-start.19 = (bf16[4,192,896]{2,1,0:T(8,128)(2,1)}, bf16[4,192,896]{2,1,0:T(8,128)(2,1)}, u32[]{:S(2)}, u32[]{:S(2)}) collective-permute-start(bf16[4,192,896]{2,1,0:T(8,128)(2,1)} %dynamic-slice_bitcast_fusion), channel_id=1, source_target_pairs={{0,4},{4,0},{8,12},{12,8},{16,20},{20,16},{24,28},{28,24},{1,5},{5... | collective-permute-start | bytes 4128776 | tf_op jit(solution)/shard_map/ppermute | solution.py:413
  286.9 33.3 %copy-start.14 = (bf16[1536,896]{1,0:T(8,128)(2,1)S(1)}, bf16[1536,896]{1,0:T(8,128)(2,1)}, u32[]{:S(2)}) copy-start(bf16[1536,896]{1,0:T(8,128)(2,1)} %copy-done.13) | copy-start | bytes 8257540
  324.4 8.5 %collective-permute-start.20 = (bf16[2,256,1536]{2,1,0:T(8,128)(2,1)}, bf16[2,256,1536]{2,1,0:T(8,128)(2,1)}, u32[]{:S(2)}, u32[]{:S(2)}) collective-permute-start(bf16[2,256,1536]{2,1,0:T(8,128)(2,1)} %select_bitcast_fusion), channel_id=1, source_target_pairs={{0,1},{1,0},{2,3},{3,2},{4,5},{5,4},{6,7},{7,6},{8,9},{9,8},{10,11... | collective-permute-start | bytes 4718600 | tf_op jit(solution)/shard_map/ppermute | solution.py:360
  328.4 16.3 %collective-permute-start.22 = (bf16[192,896]{1,0:T(8,128)(2,1)S(1)}, bf16[192,896]{1,0:T(8,128)(2,1)S(1)}, u32[]{:S(2)}, u32[]{:S(2)}) collective-permute-start(bf16[192,896]{1,0:T(8,128)(2,1)S(1)} %get-tuple-element.77), channel_id=1, source_target_pairs={{0,8},{4,12},{8,0},{12,4},{16,24},{20,28},{24,16},{28,20},{1,9},{5... | collective-permute-start | bytes 1032200 | tf_op jit(solution)/shard_map/ppermute | solution.py:413
  329.8 26.6 %collective-permute-start.23 = (bf16[192,896]{1,0:T(8,128)(2,1)S(1)}, bf16[192,896]{1,0:T(8,128)(2,1)S(1)}, u32[]{:S(2)}, u32[]{:S(2)}) collective-permute-start(bf16[192,896]{1,0:T(8,128)(2,1)S(1)} %get-tuple-element.79), channel_id=1, source_target_pairs={{0,16},{4,20},{8,24},{12,28},{16,0},{20,4},{24,8},{28,12},{1,17},{... | collective-permute-start | bytes 1032200 | tf_op jit(solution)/shard_map/ppermute | solution.py:413
  330.9 25.6 %collective-permute-start.24 = (bf16[192,896]{1,0:T(8,128)(2,1)S(1)}, bf16[192,896]{1,0:T(8,128)(2,1)S(1)}, u32[]{:S(2)}, u32[]{:S(2)}) collective-permute-start(bf16[192,896]{1,0:T(8,128)(2,1)S(1)} %get-tuple-element.78), channel_id=1, source_target_pairs={{0,24},{4,28},{8,16},{12,20},{16,8},{20,12},{24,0},{28,4},{1,25},{... | collective-permute-start | bytes 1032200 | tf_op jit(solution)/shard_map/ppermute | solution.py:413
  334.9 22.7 %copy-start.28 = (bf16[384,768]{1,0:T(8,128)(2,1)S(1)}, bf16[384,768]{1,0:T(8,128)(2,1)}, u32[]{:S(2)}) copy-start(bf16[384,768]{1,0:T(8,128)(2,1)} %reduce-scatter.3.cloned.1.call-done) | copy-start | bytes 1769476
  335.0 33.9 %collective-permute-start.21 = (bf16[1,256,1536]{2,1,0:T(8,128)(2,1)S(1)}, bf16[1,256,1536]{2,1,0:T(8,128)(2,1)S(1)}, u32[]{:S(2)}, u32[]{:S(2)}) collective-permute-start(bf16[1,256,1536]{2,1,0:T(8,128)(2,1)S(1)} %fusion.32), channel_id=1, source_target_pairs={{0,2},{1,3},{2,0},{3,1},{4,6},{5,7},{6,4},{7,5},{8,10},{9,11},{10,... | collective-permute-start | bytes 2359304 | tf_op jit(solution)/shard_map/ppermute | solution.py:360
  357.7 1.3 collective-permute-start.30
  358.4 33.0 %collective-permute-start.33 = (bf16[1,48,896]{2,1,0:T(8,128)(2,1)}, bf16[1,48,896]{2,1,0:T(8,128)(2,1)}, u32[]{:S(2)}, u32[]{:S(2)}) collective-permute-start(bf16[1,48,896]{2,1,0:T(8,128)(2,1)} %constant_dynamic-slice_fusion.2), channel_id=1, source_target_pairs={{0,1},{1,0},{2,3},{3,2},{4,5},{5,4},{6,7},{7,6},{8,9},{9,8},{10,11... | collective-permute-start | bytes 258056 | tf_op jit(solution)/shard_map/ppermute | solution.py:496
  359.0 12.7 %collective-permute-start.31 = (bf16[1,48,768]{2,1,0:T(8,128)(2,1)S(1)}, bf16[1,48,768]{2,1,0:T(8,128)(2,1)S(1)}, u32[]{:S(2)}, u32[]{:S(2)}) collective-permute-start(bf16[1,48,768]{2,1,0:T(8,128)(2,1)S(1)} %get-tuple-element.94), channel_id=1, source_target_pairs={{0,2},{1,3},{2,0},{3,1},{4,6},{5,7},{6,4},{7,5},{8,10},{9,11},{10,... | collective-permute-start | bytes 221192 | tf_op jit(solution)/shard_map/ppermute | solution.py:496
  369.3 18.2 %copy-start.1 = (bf16[1,256,1536]{2,1,0:T(8,128)(2,1)S(1)}, bf16[1,256,1536]{2,1,0:T(8,128)(2,1)}, u32[]{:S(2)}) copy-start(bf16[1,256,1536]{2,1,0:T(8,128)(2,1)} %param.12) | copy-start | bytes 2359300
  369.7 17.0 %collective-permute-start.36 = (bf16[96,1536]{1,0:T(8,128)(2,1)S(1)}, bf16[96,1536]{1,0:T(8,128)(2,1)S(1)}, u32[]{:S(2)}, u32[]{:S(2)}) collective-permute-start(bf16[96,1536]{1,0:T(8,128)(2,1)S(1)} %bitcast.257), channel_id=1, source_target_pairs={{0,0},{4,1},{8,2},{12,3},{16,4},{20,5},{24,6},{28,7},{1,8},{5,9},{... | collective-permute-start | bytes 884744 | tf_op jit(solution)/shard_map/ppermute | solution.py:663
  371.6 4.0 collective-permute-start.32
  391.4 3.9 collective-permute-start.25
  392.4 11.7 %collective-permute-start.34 = (bf16[1,48,896]{2,1,0:T(8,128)(2,1)S(1)}, bf16[1,48,896]{2,1,0:T(8,128)(2,1)S(1)}, u32[]{:S(2)}, u32[]{:S(2)}) collective-permute-start(bf16[1,48,896]{2,1,0:T(8,128)(2,1)S(1)} %get-tuple-element.91), channel_id=1, source_target_pairs={{0,2},{1,3},{2,0},{3,1},{4,6},{5,7},{6,4},{7,5},{8,10},{9,11},{10,... | collective-permute-start | bytes 258056 | tf_op jit(solution)/shard_map/ppermute | solution.py:496
  392.5 11.7 %collective-permute-start.35 = (bf16[1,48,896]{2,1,0:T(8,128)(2,1)S(1)}, bf16[1,48,896]{2,1,0:T(8,128)(2,1)S(1)}, u32[]{:S(2)}, u32[]{:S(2)}) collective-permute-start(bf16[1,48,896]{2,1,0:T(8,128)(2,1)S(1)} %get-tuple-element.90), channel_id=1, source_target_pairs={{0,3},{1,2},{2,1},{3,0},{4,7},{5,6},{6,5},{7,4},{8,11},{9,10},{10,... | collective-permute-start | bytes 258056 | tf_op jit(solution)/shard_map/ppermute | solution.py:496
  395.3 3.9 collective-permute-start.26
  399.2 4.8 %collective-permute-start.27 = (f32[6500]{0:T(1024)S(1)}, f32[6500]{0:T(1024)S(1)}, u32[]{:S(2)}, u32[]{:S(2)}) collective-permute-start(f32[6500]{0:T(1024)S(1)} %add.299), channel_id=1, source_target_pairs={{0,16},{4,20},{8,24},{12,28},{16,0},{20,4},{24,8},{28,12},{1,17},{... | collective-permute-start | bytes 78008 | tf_op jit(solution)/shard_map/ppermute | solution.py:402
  404.0 3.9 collective-permute-start.28
  408.0 1.3 collective-permute-start.29
  (33 other events, 138.0 us)
Sparse Core Ops, SparseCore 0:
  27.0 102.6 all-gather.2
  219.8 97.9 reduce-scatter.2
  323.2 50.7 reduce-scatter.4
